TPU v7x, 512 devices: a whole 4x4x16 slice. The times are simulated.
512 devices in a mesh: depth: 8 (over x, core), strip: 64 (over y, z).
Axes of the slice: x: 4, y: 4, z: 16, core: 2. Of those that a mesh axis runs over, the one named last changes fastest.
Arguments:
- surface: float32 [2, 4, 1024, 1024], P(None, None, 'strip'), may hold values from -6 to 6
- velocity_class: int32 [8, 1024, 1024], P('depth', 'strip'), may hold values from 0 to 7
- table: float32 [2, 8, 2, 10], replicated, may hold values from -2 to 2
Outputs:
- image: float32 [8, 1024, 1024], P('depth', 'strip')
All inputs are finite; a program needn't handle non-finite values.
Results may differ from a plain program's by a relative error of at most 0.00017.
Values sent between devices are 32-bit elements; how exact they have to be, the bound alone decides.
No kernel may reach another device: no remote copies, remote signals or barrier semaphores. Data moves between devices by JAX's collectives and lax.ppermute only.
A program may use at most 64 MiB of HBM per device.

v0:
```python
import jax
import jax.numpy as jnp
from jax import lax
from jax.sharding import PartitionSpec as P

PASSES = 9
CLASSES = 8


def extended(shard, sides, width):
    for axis, dim in sides:
        devices, length = (lax.axis_size(axis), shard.shape[dim])
        up = [(i, (i + 1) % devices) for i in range(devices - 1)]
        down = [(j, i) for i, j in up]
        last = lax.slice_in_dim(shard, length - width, length, axis=dim)
        initial = lax.slice_in_dim(shard, 0, width, axis=dim)
        before = lax.ppermute(last, axis, up)
        after = lax.ppermute(initial, axis, down)
        shard = jnp.concatenate([before, shard, after], axis=dim)
    return shard


def mcclellan(field):
    lead = [(0, 0)] * (field.ndim - 2)
    padded = jnp.pad(field, lead + [(1, 1), (1, 1)])
    beside = (
        padded[..., 2:, 1:-1]
        + padded[..., :-2, 1:-1]
        + padded[..., 1:-1, 2:]
        + padded[..., 1:-1, :-2]
    )
    corners = (
        padded[..., 2:, 2:] + padded[..., 2:, :-2] + padded[..., :-2, 2:] + padded[..., :-2, :-2]
    )
    return -0.5 * field + 0.25 * beside + 0.125 * corners


def weigh(result, field, real_part, imag_part):
    return jnp.stack(
        [
            result[:, 0] + (real_part * field[:, 0] - imag_part * field[:, 1]),
            result[:, 1] + (real_part * field[:, 1] + imag_part * field[:, 0]),
            result[:, 2] + (real_part * field[:, 2] + imag_part * field[:, 3]),
            result[:, 3] + (real_part * field[:, 3] - imag_part * field[:, 2]),
        ],
        axis=1,
    )


def correlate(fields):
    total = jnp.zeros(fields.shape[2:], jnp.float32)
    for freq_index in range(fields.shape[0]):
        total = total + (
            fields[freq_index, 0] * fields[freq_index, 2]
            + fields[freq_index, 1] * fields[freq_index, 3]
        )
    return total


def tile_halo(sending, rim_width):
    return extended(sending, (("depth", 4), ("strip", 3)), rim_width)


def clip_domain(field, rim_width):
    row_count = field.shape[-2] - 2 * rim_width
    row_ids = (
        lax.axis_index("strip") * row_count
        - rim_width
        + jnp.arange(field.shape[-2], dtype=jnp.int32)
    )
    keep = ((row_ids >= 0) & (row_ids < row_count * lax.axis_size("strip")))[:, None]
    col_count = field.shape[-1] - 2 * rim_width
    col_ids = (
        lax.axis_index("depth") * col_count
        - rim_width
        + jnp.arange(field.shape[-1], dtype=jnp.int32)
    )
    keep = keep & ((col_ids >= 0) & (col_ids < col_count * lax.axis_size("depth")))[None, :]
    return jnp.where(keep, field, 0.0)


def chebyshev(fields, onehot, table_part, rim_width, widen):
    row_count = fields.shape[-2]
    col_count = fields.shape[-1]

    def own_cells(field):
        inner = field[..., rim_width : rim_width + row_count, :]
        inner = inner[..., rim_width : rim_width + col_count]
        return inner

    def coefficients(degree):
        pair = jnp.einsum(
            "cij,fcp->fpij", onehot, table_part[:, :, :, degree], precision=lax.Precision.HIGHEST
        )
        return (pair[:, 0], pair[:, 1])

    real_part, imag_part = coefficients(0)
    result = weigh(jnp.zeros_like(fields), fields, real_part, imag_part)
    previous = fields
    current = fields
    for block_index in range(PASSES // rim_width):
        sending = current[None] if block_index == 0 else jnp.stack([previous, current])
        widened = widen(sending, rim_width)
        wide_prev = widened[0]
        wide_curr = widened[-1]
        for inner_pass in range(rim_width):
            degree = block_index * rim_width + inner_pass
            if degree == 0:
                following = mcclellan(wide_curr)
            else:
                following = 2.0 * mcclellan(wide_curr) - wide_prev
            following = clip_domain(following, rim_width)
            wide_prev, wide_curr = (wide_curr, following)
            real_part, imag_part = coefficients(degree + 1)
            result = weigh(result, own_cells(wide_curr), real_part, imag_part)
        previous = own_cells(wide_prev)
        current = own_cells(wide_curr)
    return result


def body(surface, velocity_class, table):
    classes = jnp.arange(CLASSES, dtype=jnp.int32)
    rim_width = 3
    velocity = lax.all_to_all(velocity_class, "depth", split_axis=2, concat_axis=0, tiled=True)
    col_count = velocity.shape[2]
    fields = lax.dynamic_slice_in_dim(surface, lax.axis_index("depth") * col_count, col_count, 3)

    def descend(level_index, state_pair):
        level_fields, image = state_pair
        classes_here = lax.dynamic_index_in_dim(velocity, level_index, 0, keepdims=False)
        onehot = (classes_here[None] == classes[:, None, None]).astype(jnp.float32)
        level_fields = chebyshev(level_fields, onehot, table, rim_width, tile_halo)
        image = lax.dynamic_update_index_in_dim(image, correlate(level_fields), level_index, 0)
        return (level_fields, image)

    initial = (fields, jnp.zeros((velocity.shape[0], velocity.shape[1], col_count), jnp.float32))
    fields, image = lax.fori_loop(0, velocity.shape[0], descend, initial)
    return lax.all_to_all(image, "depth", split_axis=0, concat_axis=2, tiled=True)


def solution(mesh):
    in_specs = (P(None, None, "strip", None), P("depth", "strip", None), P())
    out_specs = P("depth", "strip", None)
    return jax.shard_map(body, mesh=mesh, in_specs=in_specs, out_specs=out_specs, check_vma=False)
```

profile of v0, /device:TPU:24, one launch (start us, length us, event | category | flops | bytes accessed | tf_op | source)
XLA Modules:
  0.0 554.1 jit_solution(4502682108848891029)
XLA Ops:
  4.6 4.3 all-to-all-start
  9.7 4.8 all-to-all-done
  16.5 522.7 %while.19 = (s32[]{:T(128)}, f32[2,4,16,128]{3,1,0,2:T(4,128)S(1)}, f32[8,16,128]{2,1,0:T(8,128)S(1)}, s32[8,16,128]{2,0,1:T(8,128)S(1)}, f32[2,8,2,10]{1,2,0,3:...) while((s32[]{:T(128)}, f32[2,4,16,128]{3,1,0,2:T(4,128)S(1)}, ...), condition=%wide.region_1.2_spmd.clone, body=%wide.region_0.1_spmd.clone.sunk | while | flops 12695103 | bytes 9011121 | solution.py:137
  22.6 11.6 %collective-permute-start.2 = (f32[1,2,4,3,134]{4,2,1,3,0:T(4,128)S(1)}, f32[1,2,4,3,134]{4,2,1,3,0:T(4,128)S(1)}, u32[]{:S(2)}, u32[]{:S(2)}) collective-permute-start(f32[1,2,4,3,134]{4,2,1,3,0:T(4,128)S(1)} %get-tuple-element.279), channel_id=1, source_target_pairs={{1,0},{2,1},{3,2},{4,3},{5,4},{6,5},{7,6},{8,7},{9,8},{10,9},{11,1... | collective-permute-start | bytes 38600 | tf_op jit(solution)/shard_map/while/body/eval_jaxpr/ppermute | solution.py:18
  36.2 5.8 %collective-permute-done.3 = f32[1,2,4,3,134]{4,2,1,3,0:T(4,128)S(1)} collective-permute-done((f32[1,2,4,3,134]{4,2,1,3,0:T(4,128)S(1)}, f32[1,2,4,3,134]{4,2,1,3,0:T(4,128)S(1)}, u32[]{:S(2)}, u32[]{:S(2)}) %collective-permute-start.3) | collective-permute-done | bytes 12896 | tf_op jit(solution)/shard_map/while/body/eval_jaxpr/ppermute | solution.py:17
  52.3 3.9 collective-permute-start.7
  56.5 4.0 collective-permute-done.7
  64.2 5.2 collective-permute-start.9
  72.4 3.9 collective-permute-start.11
  76.6 4.0 collective-permute-done.11
  87.1 5.9 %collective-permute-start.1 = (f32[1,2,4,16,3]{4,2,1,3,0:T(4,128)S(1)}, f32[1,2,4,16,3]{4,2,1,3,0:T(4,128)S(1)}, u32[]{:S(2)}, u32[]{:S(2)}) collective-permute-start(f32[1,2,4,16,3]{4,2,1,3,0:T(4,128)S(1)} %get-tuple-element.278), channel_id=1, source_target_pairs={{0,64},{64,128},{128,192},{192,256},{256,320},{320,384},{384,448},... | collective-permute-start | bytes 4616 | tf_op jit(solution)/shard_map/while/body/eval_jaxpr/ppermute | solution.py:17
  96.3 3.9 collective-permute-start.3
  108.4 5.0 collective-permute-start.5
  116.5 3.9 collective-permute-start.7
  120.6 4.0 collective-permute-done.7
  128.3 5.9 %collective-permute-start.9 = (f32[2,2,4,16,3]{4,2,1,3,0:T(4,128)S(1)}, f32[2,2,4,16,3]{4,2,1,3,0:T(4,128)S(1)}, u32[]{:S(2)}, u32[]{:S(2)}) collective-permute-start(f32[2,2,4,16,3]{4,2,1,3,0:T(4,128)S(1)} %get-tuple-element.288), channel_id=1, source_target_pairs={{0,64},{64,128},{128,192},{192,256},{256,320},{320,384},{384,448},... | collective-permute-start | bytes 9224 | tf_op jit(solution)/shard_map/while/body/eval_jaxpr/ppermute | solution.py:17
  137.2 3.9 collective-permute-start.11
  141.4 4.0 collective-permute-done.11
  151.9 5.9 %collective-permute-start.1 = (f32[1,2,4,16,3]{4,2,1,3,0:T(4,128)S(1)}, f32[1,2,4,16,3]{4,2,1,3,0:T(4,128)S(1)}, u32[]{:S(2)}, u32[]{:S(2)}) collective-permute-start(f32[1,2,4,16,3]{4,2,1,3,0:T(4,128)S(1)} %get-tuple-element.278), channel_id=1, source_target_pairs={{0,64},{64,128},{128,192},{192,256},{256,320},{320,384},{384,448},... | collective-permute-start | bytes 4616 | tf_op jit(solution)/shard_map/while/body/eval_jaxpr/ppermute | solution.py:17
  161.1 3.9 collective-permute-start.3
  173.2 5.0 collective-permute-start.5
  181.3 3.9 collective-permute-start.7
  185.4 4.0 collective-permute-done.7
  193.1 5.9 %collective-permute-start.9 = (f32[2,2,4,16,3]{4,2,1,3,0:T(4,128)S(1)}, f32[2,2,4,16,3]{4,2,1,3,0:T(4,128)S(1)}, u32[]{:S(2)}, u32[]{:S(2)}) collective-permute-start(f32[2,2,4,16,3]{4,2,1,3,0:T(4,128)S(1)} %get-tuple-element.288), channel_id=1, source_target_pairs={{0,64},{64,128},{128,192},{192,256},{256,320},{320,384},{384,448},... | collective-permute-start | bytes 9224 | tf_op jit(solution)/shard_map/while/body/eval_jaxpr/ppermute | solution.py:17
  202.0 3.9 collective-permute-start.11
  206.2 4.0 collective-permute-done.11
  216.7 5.9 %collective-permute-start.1 = (f32[1,2,4,16,3]{4,2,1,3,0:T(4,128)S(1)}, f32[1,2,4,16,3]{4,2,1,3,0:T(4,128)S(1)}, u32[]{:S(2)}, u32[]{:S(2)}) collective-permute-start(f32[1,2,4,16,3]{4,2,1,3,0:T(4,128)S(1)} %get-tuple-element.278), channel_id=1, source_target_pairs={{0,64},{64,128},{128,192},{192,256},{256,320},{320,384},{384,448},... | collective-permute-start | bytes 4616 | tf_op jit(solution)/shard_map/while/body/eval_jaxpr/ppermute | solution.py:17
  225.9 3.9 collective-permute-start.3
  238.0 5.0 collective-permute-start.5
  246.1 3.9 collective-permute-start.7
  250.2 4.0 collective-permute-done.7
  257.9 5.9 %collective-permute-start.9 = (f32[2,2,4,16,3]{4,2,1,3,0:T(4,128)S(1)}, f32[2,2,4,16,3]{4,2,1,3,0:T(4,128)S(1)}, u32[]{:S(2)}, u32[]{:S(2)}) collective-permute-start(f32[2,2,4,16,3]{4,2,1,3,0:T(4,128)S(1)} %get-tuple-element.288), channel_id=1, source_target_pairs={{0,64},{64,128},{128,192},{192,256},{256,320},{320,384},{384,448},... | collective-permute-start | bytes 9224 | tf_op jit(solution)/shard_map/while/body/eval_jaxpr/ppermute | solution.py:17
  266.8 3.9 collective-permute-start.11
  271.0 4.0 collective-permute-done.11
  281.5 5.9 %collective-permute-start.1 = (f32[1,2,4,16,3]{4,2,1,3,0:T(4,128)S(1)}, f32[1,2,4,16,3]{4,2,1,3,0:T(4,128)S(1)}, u32[]{:S(2)}, u32[]{:S(2)}) collective-permute-start(f32[1,2,4,16,3]{4,2,1,3,0:T(4,128)S(1)} %get-tuple-element.278), channel_id=1, source_target_pairs={{0,64},{64,128},{128,192},{192,256},{256,320},{320,384},{384,448},... | collective-permute-start | bytes 4616 | tf_op jit(solution)/shard_map/while/body/eval_jaxpr/ppermute | solution.py:17
  290.7 3.9 collective-permute-start.3
  302.8 5.0 collective-permute-start.5
  310.9 3.9 collective-permute-start.7
  315.0 4.0 collective-permute-done.7
  322.7 5.9 %collective-permute-start.9 = (f32[2,2,4,16,3]{4,2,1,3,0:T(4,128)S(1)}, f32[2,2,4,16,3]{4,2,1,3,0:T(4,128)S(1)}, u32[]{:S(2)}, u32[]{:S(2)}) collective-permute-start(f32[2,2,4,16,3]{4,2,1,3,0:T(4,128)S(1)} %get-tuple-element.288), channel_id=1, source_target_pairs={{0,64},{64,128},{128,192},{192,256},{256,320},{320,384},{384,448},... | collective-permute-start | bytes 9224 | tf_op jit(solution)/shard_map/while/body/eval_jaxpr/ppermute | solution.py:17
  331.6 3.9 collective-permute-start.11
  335.8 4.0 collective-permute-done.11
  346.3 5.9 %collective-permute-start.1 = (f32[1,2,4,16,3]{4,2,1,3,0:T(4,128)S(1)}, f32[1,2,4,16,3]{4,2,1,3,0:T(4,128)S(1)}, u32[]{:S(2)}, u32[]{:S(2)}) collective-permute-start(f32[1,2,4,16,3]{4,2,1,3,0:T(4,128)S(1)} %get-tuple-element.278), channel_id=1, source_target_pairs={{0,64},{64,128},{128,192},{192,256},{256,320},{320,384},{384,448},... | collective-permute-start | bytes 4616 | tf_op jit(solution)/shard_map/while/body/eval_jaxpr/ppermute | solution.py:17
  355.5 3.9 collective-permute-start.3
  367.6 5.0 collective-permute-start.5
  379.8 4.0 collective-permute-done.7
  387.5 5.9 %collective-permute-start.9 = (f32[2,2,4,16,3]{4,2,1,3,0:T(4,128)S(1)}, f32[2,2,4,16,3]{4,2,1,3,0:T(4,128)S(1)}, u32[]{:S(2)}, u32[]{:S(2)}) collective-permute-start(f32[2,2,4,16,3]{4,2,1,3,0:T(4,128)S(1)} %get-tuple-element.288), channel_id=1, source_target_pairs={{0,64},{64,128},{128,192},{192,256},{256,320},{320,384},{384,448},... | collective-permute-start | bytes 9224 | tf_op jit(solution)/shard_map/while/body/eval_jaxpr/ppermute | solution.py:17
  396.4 3.9 collective-permute-start.11
  400.6 4.0 collective-permute-done.11
  411.0 5.9 %collective-permute-start.1 = (f32[1,2,4,16,3]{4,2,1,3,0:T(4,128)S(1)}, f32[1,2,4,16,3]{4,2,1,3,0:T(4,128)S(1)}, u32[]{:S(2)}, u32[]{:S(2)}) collective-permute-start(f32[1,2,4,16,3]{4,2,1,3,0:T(4,128)S(1)} %get-tuple-element.278), channel_id=1, source_target_pairs={{0,64},{64,128},{128,192},{192,256},{256,320},{320,384},{384,448},... | collective-permute-start | bytes 4616 | tf_op jit(solution)/shard_map/while/body/eval_jaxpr/ppermute | solution.py:17
  420.3 3.9 collective-permute-start.3
  432.4 5.0 collective-permute-start.5
  444.6 4.0 collective-permute-done.7
  452.3 5.9 %collective-permute-start.9 = (f32[2,2,4,16,3]{4,2,1,3,0:T(4,128)S(1)}, f32[2,2,4,16,3]{4,2,1,3,0:T(4,128)S(1)}, u32[]{:S(2)}, u32[]{:S(2)}) collective-permute-start(f32[2,2,4,16,3]{4,2,1,3,0:T(4,128)S(1)} %get-tuple-element.288), channel_id=1, source_target_pairs={{0,64},{64,128},{128,192},{192,256},{256,320},{320,384},{384,448},... | collective-permute-start | bytes 9224 | tf_op jit(solution)/shard_map/while/body/eval_jaxpr/ppermute | solution.py:17
  461.2 3.9 collective-permute-start.11
  465.4 4.0 collective-permute-done.11
  475.8 5.9 %collective-permute-start.1 = (f32[1,2,4,16,3]{4,2,1,3,0:T(4,128)S(1)}, f32[1,2,4,16,3]{4,2,1,3,0:T(4,128)S(1)}, u32[]{:S(2)}, u32[]{:S(2)}) collective-permute-start(f32[1,2,4,16,3]{4,2,1,3,0:T(4,128)S(1)} %get-tuple-element.278), channel_id=1, source_target_pairs={{0,64},{64,128},{128,192},{192,256},{256,320},{320,384},{384,448},... | collective-permute-start | bytes 4616 | tf_op jit(solution)/shard_map/while/body/eval_jaxpr/ppermute | solution.py:17
  485.1 3.9 collective-permute-start.3
  497.2 5.0 collective-permute-start.5
  509.4 4.0 collective-permute-done.7
  517.1 5.9 %collective-permute-start.9 = (f32[2,2,4,16,3]{4,2,1,3,0:T(4,128)S(1)}, f32[2,2,4,16,3]{4,2,1,3,0:T(4,128)S(1)}, u32[]{:S(2)}, u32[]{:S(2)}) collective-permute-start(f32[2,2,4,16,3]{4,2,1,3,0:T(4,128)S(1)} %get-tuple-element.288), channel_id=1, source_target_pairs={{0,64},{64,128},{128,192},{192,256},{256,320},{320,384},{384,448},... | collective-permute-start | bytes 9224 | tf_op jit(solution)/shard_map/while/body/eval_jaxpr/ppermute | solution.py:17
  526.0 3.9 collective-permute-start.11
  530.2 4.0 collective-permute-done.11
  539.2 14.2 %all_to_all.36 = f32[8,16,128]{2,1,0:T(8,128)S(1)} all-to-all(f32[8,16,128]{2,1,0:T(8,128)S(1)} %get-tuple-element.180), channel_id=1, replica_groups=mesh['depth'=8,'strip'=64] {'depth'}, dimensions={0} | all-to-all | bytes 131072 | tf_op jit(solution)/shard_map/all_to_all | solution.py:138
  (500 shorter events, 244.9 us)
Async XLA Ops:
  4.6 9.9 %all-to-all-start = ((s32[8,1,2048]{2,1,0:T(1,128)}), s32[8,1,2048]{2,1,0:T(1,128)S(1)}, u32[]{:S(2)}, u32[]{:S(2)}) async-start(s32[8,1,2048]{2,1,0:T(1,128)} %reshape.214), calls=%async_computation | async-start | bytes 131072 | tf_op jit(solution)/shard_map/all_to_all | solution.py:124
  22.6 13.6 %collective-permute-start.2 = (f32[1,2,4,3,134]{4,2,1,3,0:T(4,128)S(1)}, f32[1,2,4,3,134]{4,2,1,3,0:T(4,128)S(1)}, u32[]{:S(2)}, u32[]{:S(2)}) collective-permute-start(f32[1,2,4,3,134]{4,2,1,3,0:T(4,128)S(1)} %get-tuple-element.279), channel_id=1, source_target_pairs={{1,0},{2,1},{3,2},{4,3},{5,4},{6,5},{7,6},{8,7},{9,8},{10,9},{11,1... | collective-permute-start | bytes 38600 | tf_op jit(solution)/shard_map/while/body/eval_jaxpr/ppermute | solution.py:18
  34.2 7.8 %collective-permute-start.3 = (f32[1,2,4,3,134]{4,2,1,3,0:T(4,128)S(1)}, f32[1,2,4,3,134]{4,2,1,3,0:T(4,128)S(1)}, u32[]{:S(2)}, u32[]{:S(2)}) collective-permute-start(f32[1,2,4,3,134]{4,2,1,3,0:T(4,128)S(1)} %get-tuple-element.280), channel_id=1, source_target_pairs={{0,1},{1,2},{2,3},{3,4},{4,5},{5,6},{6,7},{7,8},{8,9},{9,10},{10,1... | collective-permute-start | bytes 38600 | tf_op jit(solution)/shard_map/while/body/eval_jaxpr/ppermute | solution.py:17
  52.3 8.1 %collective-permute-start.7 = (f32[2,2,4,3,134]{4,2,1,3,0:T(4,128)S(1)}, f32[2,2,4,3,134]{4,2,1,3,0:T(4,128)S(1)}, u32[]{:S(2)}, u32[]{:S(2)}) collective-permute-start(f32[2,2,4,3,134]{4,2,1,3,0:T(4,128)S(1)} %get-tuple-element.286), channel_id=1, source_target_pairs={{0,1},{1,2},{2,3},{3,4},{4,5},{5,6},{6,7},{7,8},{8,9},{9,10},{10,1... | collective-permute-start | bytes 77192 | tf_op jit(solution)/shard_map/while/body/eval_jaxpr/ppermute | solution.py:17
  62.9 6.7 %collective-permute-start.8 = (f32[2,2,4,16,3]{4,2,1,3,0:T(4,128)S(1)}, f32[2,2,4,16,3]{4,2,1,3,0:T(4,128)S(1)}, u32[]{:S(2)}, u32[]{:S(2)}) collective-permute-start(f32[2,2,4,16,3]{4,2,1,3,0:T(4,128)S(1)} %get-tuple-element.287), channel_id=1, source_target_pairs={{64,0},{128,64},{192,128},{256,192},{320,256},{384,320},{448,384},... | collective-permute-start | bytes 9224 | tf_op jit(solution)/shard_map/while/body/eval_jaxpr/ppermute | solution.py:18
  64.2 6.2 %collective-permute-start.9 = (f32[2,2,4,16,3]{4,2,1,3,0:T(4,128)S(1)}, f32[2,2,4,16,3]{4,2,1,3,0:T(4,128)S(1)}, u32[]{:S(2)}, u32[]{:S(2)}) collective-permute-start(f32[2,2,4,16,3]{4,2,1,3,0:T(4,128)S(1)} %get-tuple-element.288), channel_id=1, source_target_pairs={{0,64},{64,128},{128,192},{192,256},{256,320},{320,384},{384,448},... | collective-permute-start | bytes 9224 | tf_op jit(solution)/shard_map/while/body/eval_jaxpr/ppermute | solution.py:17
  70.5 6.1 %collective-permute-start.10 = (f32[2,2,4,3,134]{4,2,1,3,0:T(4,128)S(1)}, f32[2,2,4,3,134]{4,2,1,3,0:T(4,128)S(1)}, u32[]{:S(2)}, u32[]{:S(2)}) collective-permute-start(f32[2,2,4,3,134]{4,2,1,3,0:T(4,128)S(1)} %get-tuple-element.289), channel_id=1, source_target_pairs={{1,0},{2,1},{3,2},{4,3},{5,4},{6,5},{7,6},{8,7},{9,8},{10,9},{11,1... | collective-permute-start | bytes 77192 | tf_op jit(solution)/shard_map/while/body/eval_jaxpr/ppermute | solution.py:18
  72.4 8.1 %collective-permute-start.11 = (f32[2,2,4,3,134]{4,2,1,3,0:T(4,128)S(1)}, f32[2,2,4,3,134]{4,2,1,3,0:T(4,128)S(1)}, u32[]{:S(2)}, u32[]{:S(2)}) collective-permute-start(f32[2,2,4,3,134]{4,2,1,3,0:T(4,128)S(1)} %get-tuple-element.290), channel_id=1, source_target_pairs={{0,1},{1,2},{2,3},{3,4},{4,5},{5,6},{6,7},{7,8},{8,9},{9,10},{10,1... | collective-permute-start | bytes 77192 | tf_op jit(solution)/shard_map/while/body/eval_jaxpr/ppermute | solution.py:17
  85.8 8.5 %collective-permute-start = (f32[1,2,4,16,3]{4,2,1,3,0:T(4,128)S(1)}, f32[1,2,4,16,3]{4,2,1,3,0:T(4,128)S(1)}, u32[]{:S(2)}, u32[]{:S(2)}) collective-permute-start(f32[1,2,4,16,3]{4,2,1,3,0:T(4,128)S(1)} %get-tuple-element.277), channel_id=1, source_target_pairs={{64,0},{128,64},{192,128},{256,192},{320,256},{384,320},{448,384},... | collective-permute-start | bytes 4616 | tf_op jit(solution)/shard_map/while/body/eval_jaxpr/ppermute | solution.py:18
  87.1 7.2 %collective-permute-start.1 = (f32[1,2,4,16,3]{4,2,1,3,0:T(4,128)S(1)}, f32[1,2,4,16,3]{4,2,1,3,0:T(4,128)S(1)}, u32[]{:S(2)}, u32[]{:S(2)}) collective-permute-start(f32[1,2,4,16,3]{4,2,1,3,0:T(4,128)S(1)} %get-tuple-element.278), channel_id=1, source_target_pairs={{0,64},{64,128},{128,192},{192,256},{256,320},{320,384},{384,448},... | collective-permute-start | bytes 4616 | tf_op jit(solution)/shard_map/while/body/eval_jaxpr/ppermute | solution.py:17
  96.3 7.8 %collective-permute-start.3 = (f32[1,2,4,3,134]{4,2,1,3,0:T(4,128)S(1)}, f32[1,2,4,3,134]{4,2,1,3,0:T(4,128)S(1)}, u32[]{:S(2)}, u32[]{:S(2)}) collective-permute-start(f32[1,2,4,3,134]{4,2,1,3,0:T(4,128)S(1)} %get-tuple-element.280), channel_id=1, source_target_pairs={{0,1},{1,2},{2,3},{3,4},{4,5},{5,6},{6,7},{7,8},{8,9},{9,10},{10,1... | collective-permute-start | bytes 38600 | tf_op jit(solution)/shard_map/while/body/eval_jaxpr/ppermute | solution.py:17
  107.1 6.5 %collective-permute-start.4 = (f32[2,2,4,16,3]{4,2,1,3,0:T(4,128)S(1)}, f32[2,2,4,16,3]{4,2,1,3,0:T(4,128)S(1)}, u32[]{:S(2)}, u32[]{:S(2)}) collective-permute-start(f32[2,2,4,16,3]{4,2,1,3,0:T(4,128)S(1)} %get-tuple-element.283), channel_id=1, source_target_pairs={{64,0},{128,64},{192,128},{256,192},{320,256},{384,320},{448,384},... | collective-permute-start | bytes 9224 | tf_op jit(solution)/shard_map/while/body/eval_jaxpr/ppermute | solution.py:18
  116.5 8.1 %collective-permute-start.7 = (f32[2,2,4,3,134]{4,2,1,3,0:T(4,128)S(1)}, f32[2,2,4,3,134]{4,2,1,3,0:T(4,128)S(1)}, u32[]{:S(2)}, u32[]{:S(2)}) collective-permute-start(f32[2,2,4,3,134]{4,2,1,3,0:T(4,128)S(1)} %get-tuple-element.286), channel_id=1, source_target_pairs={{0,1},{1,2},{2,3},{3,4},{4,5},{5,6},{6,7},{7,8},{8,9},{9,10},{10,1... | collective-permute-start | bytes 77192 | tf_op jit(solution)/shard_map/while/body/eval_jaxpr/ppermute | solution.py:17
  127.0 7.4 %collective-permute-start.8 = (f32[2,2,4,16,3]{4,2,1,3,0:T(4,128)S(1)}, f32[2,2,4,16,3]{4,2,1,3,0:T(4,128)S(1)}, u32[]{:S(2)}, u32[]{:S(2)}) collective-permute-start(f32[2,2,4,16,3]{4,2,1,3,0:T(4,128)S(1)} %get-tuple-element.287), channel_id=1, source_target_pairs={{64,0},{128,64},{192,128},{256,192},{320,256},{384,320},{448,384},... | collective-permute-start | bytes 9224 | tf_op jit(solution)/shard_map/while/body/eval_jaxpr/ppermute | solution.py:18
  128.3 6.8 %collective-permute-start.9 = (f32[2,2,4,16,3]{4,2,1,3,0:T(4,128)S(1)}, f32[2,2,4,16,3]{4,2,1,3,0:T(4,128)S(1)}, u32[]{:S(2)}, u32[]{:S(2)}) collective-permute-start(f32[2,2,4,16,3]{4,2,1,3,0:T(4,128)S(1)} %get-tuple-element.288), channel_id=1, source_target_pairs={{0,64},{64,128},{128,192},{192,256},{256,320},{320,384},{384,448},... | collective-permute-start | bytes 9224 | tf_op jit(solution)/shard_map/while/body/eval_jaxpr/ppermute | solution.py:17
  137.2 8.1 %collective-permute-start.11 = (f32[2,2,4,3,134]{4,2,1,3,0:T(4,128)S(1)}, f32[2,2,4,3,134]{4,2,1,3,0:T(4,128)S(1)}, u32[]{:S(2)}, u32[]{:S(2)}) collective-permute-start(f32[2,2,4,3,134]{4,2,1,3,0:T(4,128)S(1)} %get-tuple-element.290), channel_id=1, source_target_pairs={{0,1},{1,2},{2,3},{3,4},{4,5},{5,6},{6,7},{7,8},{8,9},{9,10},{10,1... | collective-permute-start | bytes 77192 | tf_op jit(solution)/shard_map/while/body/eval_jaxpr/ppermute | solution.py:17
  150.6 8.5 %collective-permute-start = (f32[1,2,4,16,3]{4,2,1,3,0:T(4,128)S(1)}, f32[1,2,4,16,3]{4,2,1,3,0:T(4,128)S(1)}, u32[]{:S(2)}, u32[]{:S(2)}) collective-permute-start(f32[1,2,4,16,3]{4,2,1,3,0:T(4,128)S(1)} %get-tuple-element.277), channel_id=1, source_target_pairs={{64,0},{128,64},{192,128},{256,192},{320,256},{384,320},{448,384},... | collective-permute-start | bytes 4616 | tf_op jit(solution)/shard_map/while/body/eval_jaxpr/ppermute | solution.py:18
  151.9 7.2 %collective-permute-start.1 = (f32[1,2,4,16,3]{4,2,1,3,0:T(4,128)S(1)}, f32[1,2,4,16,3]{4,2,1,3,0:T(4,128)S(1)}, u32[]{:S(2)}, u32[]{:S(2)}) collective-permute-start(f32[1,2,4,16,3]{4,2,1,3,0:T(4,128)S(1)} %get-tuple-element.278), channel_id=1, source_target_pairs={{0,64},{64,128},{128,192},{192,256},{256,320},{320,384},{384,448},... | collective-permute-start | bytes 4616 | tf_op jit(solution)/shard_map/while/body/eval_jaxpr/ppermute | solution.py:17
  161.1 7.8 %collective-permute-start.3 = (f32[1,2,4,3,134]{4,2,1,3,0:T(4,128)S(1)}, f32[1,2,4,3,134]{4,2,1,3,0:T(4,128)S(1)}, u32[]{:S(2)}, u32[]{:S(2)}) collective-permute-start(f32[1,2,4,3,134]{4,2,1,3,0:T(4,128)S(1)} %get-tuple-element.280), channel_id=1, source_target_pairs={{0,1},{1,2},{2,3},{3,4},{4,5},{5,6},{6,7},{7,8},{8,9},{9,10},{10,1... | collective-permute-start | bytes 38600 | tf_op jit(solution)/shard_map/while/body/eval_jaxpr/ppermute | solution.py:17
  171.9 6.5 %collective-permute-start.4 = (f32[2,2,4,16,3]{4,2,1,3,0:T(4,128)S(1)}, f32[2,2,4,16,3]{4,2,1,3,0:T(4,128)S(1)}, u32[]{:S(2)}, u32[]{:S(2)}) collective-permute-start(f32[2,2,4,16,3]{4,2,1,3,0:T(4,128)S(1)} %get-tuple-element.283), channel_id=1, source_target_pairs={{64,0},{128,64},{192,128},{256,192},{320,256},{384,320},{448,384},... | collective-permute-start | bytes 9224 | tf_op jit(solution)/shard_map/while/body/eval_jaxpr/ppermute | solution.py:18
  181.3 8.1 %collective-permute-start.7 = (f32[2,2,4,3,134]{4,2,1,3,0:T(4,128)S(1)}, f32[2,2,4,3,134]{4,2,1,3,0:T(4,128)S(1)}, u32[]{:S(2)}, u32[]{:S(2)}) collective-permute-start(f32[2,2,4,3,134]{4,2,1,3,0:T(4,128)S(1)} %get-tuple-element.286), channel_id=1, source_target_pairs={{0,1},{1,2},{2,3},{3,4},{4,5},{5,6},{6,7},{7,8},{8,9},{9,10},{10,1... | collective-permute-start | bytes 77192 | tf_op jit(solution)/shard_map/while/body/eval_jaxpr/ppermute | solution.py:17
  191.8 7.4 %collective-permute-start.8 = (f32[2,2,4,16,3]{4,2,1,3,0:T(4,128)S(1)}, f32[2,2,4,16,3]{4,2,1,3,0:T(4,128)S(1)}, u32[]{:S(2)}, u32[]{:S(2)}) collective-permute-start(f32[2,2,4,16,3]{4,2,1,3,0:T(4,128)S(1)} %get-tuple-element.287), channel_id=1, source_target_pairs={{64,0},{128,64},{192,128},{256,192},{320,256},{384,320},{448,384},... | collective-permute-start | bytes 9224 | tf_op jit(solution)/shard_map/while/body/eval_jaxpr/ppermute | solution.py:18
  193.1 6.8 %collective-permute-start.9 = (f32[2,2,4,16,3]{4,2,1,3,0:T(4,128)S(1)}, f32[2,2,4,16,3]{4,2,1,3,0:T(4,128)S(1)}, u32[]{:S(2)}, u32[]{:S(2)}) collective-permute-start(f32[2,2,4,16,3]{4,2,1,3,0:T(4,128)S(1)} %get-tuple-element.288), channel_id=1, source_target_pairs={{0,64},{64,128},{128,192},{192,256},{256,320},{320,384},{384,448},... | collective-permute-start | bytes 9224 | tf_op jit(solution)/shard_map/while/body/eval_jaxpr/ppermute | solution.py:17
  202.0 8.1 %collective-permute-start.11 = (f32[2,2,4,3,134]{4,2,1,3,0:T(4,128)S(1)}, f32[2,2,4,3,134]{4,2,1,3,0:T(4,128)S(1)}, u32[]{:S(2)}, u32[]{:S(2)}) collective-permute-start(f32[2,2,4,3,134]{4,2,1,3,0:T(4,128)S(1)} %get-tuple-element.290), channel_id=1, source_target_pairs={{0,1},{1,2},{2,3},{3,4},{4,5},{5,6},{6,7},{7,8},{8,9},{9,10},{10,1... | collective-permute-start | bytes 77192 | tf_op jit(solution)/shard_map/while/body/eval_jaxpr/ppermute | solution.py:17
  215.4 8.5 %collective-permute-start = (f32[1,2,4,16,3]{4,2,1,3,0:T(4,128)S(1)}, f32[1,2,4,16,3]{4,2,1,3,0:T(4,128)S(1)}, u32[]{:S(2)}, u32[]{:S(2)}) collective-permute-start(f32[1,2,4,16,3]{4,2,1,3,0:T(4,128)S(1)} %get-tuple-element.277), channel_id=1, source_target_pairs={{64,0},{128,64},{192,128},{256,192},{320,256},{384,320},{448,384},... | collective-permute-start | bytes 4616 | tf_op jit(solution)/shard_map/while/body/eval_jaxpr/ppermute | solution.py:18
  216.7 7.2 %collective-permute-start.1 = (f32[1,2,4,16,3]{4,2,1,3,0:T(4,128)S(1)}, f32[1,2,4,16,3]{4,2,1,3,0:T(4,128)S(1)}, u32[]{:S(2)}, u32[]{:S(2)}) collective-permute-start(f32[1,2,4,16,3]{4,2,1,3,0:T(4,128)S(1)} %get-tuple-element.278), channel_id=1, source_target_pairs={{0,64},{64,128},{128,192},{192,256},{256,320},{320,384},{384,448},... | collective-permute-start | bytes 4616 | tf_op jit(solution)/shard_map/while/body/eval_jaxpr/ppermute | solution.py:17
  225.9 7.8 %collective-permute-start.3 = (f32[1,2,4,3,134]{4,2,1,3,0:T(4,128)S(1)}, f32[1,2,4,3,134]{4,2,1,3,0:T(4,128)S(1)}, u32[]{:S(2)}, u32[]{:S(2)}) collective-permute-start(f32[1,2,4,3,134]{4,2,1,3,0:T(4,128)S(1)} %get-tuple-element.280), channel_id=1, source_target_pairs={{0,1},{1,2},{2,3},{3,4},{4,5},{5,6},{6,7},{7,8},{8,9},{9,10},{10,1... | collective-permute-start | bytes 38600 | tf_op jit(solution)/shard_map/while/body/eval_jaxpr/ppermute | solution.py:17
  236.7 6.5 %collective-permute-start.4 = (f32[2,2,4,16,3]{4,2,1,3,0:T(4,128)S(1)}, f32[2,2,4,16,3]{4,2,1,3,0:T(4,128)S(1)}, u32[]{:S(2)}, u32[]{:S(2)}) collective-permute-start(f32[2,2,4,16,3]{4,2,1,3,0:T(4,128)S(1)} %get-tuple-element.283), channel_id=1, source_target_pairs={{64,0},{128,64},{192,128},{256,192},{320,256},{384,320},{448,384},... | collective-permute-start | bytes 9224 | tf_op jit(solution)/shard_map/while/body/eval_jaxpr/ppermute | solution.py:18
  246.1 8.1 %collective-permute-start.7 = (f32[2,2,4,3,134]{4,2,1,3,0:T(4,128)S(1)}, f32[2,2,4,3,134]{4,2,1,3,0:T(4,128)S(1)}, u32[]{:S(2)}, u32[]{:S(2)}) collective-permute-start(f32[2,2,4,3,134]{4,2,1,3,0:T(4,128)S(1)} %get-tuple-element.286), channel_id=1, source_target_pairs={{0,1},{1,2},{2,3},{3,4},{4,5},{5,6},{6,7},{7,8},{8,9},{9,10},{10,1... | collective-permute-start | bytes 77192 | tf_op jit(solution)/shard_map/while/body/eval_jaxpr/ppermute | solution.py:17
  256.6 7.4 %collective-permute-start.8 = (f32[2,2,4,16,3]{4,2,1,3,0:T(4,128)S(1)}, f32[2,2,4,16,3]{4,2,1,3,0:T(4,128)S(1)}, u32[]{:S(2)}, u32[]{:S(2)}) collective-permute-start(f32[2,2,4,16,3]{4,2,1,3,0:T(4,128)S(1)} %get-tuple-element.287), channel_id=1, source_target_pairs={{64,0},{128,64},{192,128},{256,192},{320,256},{384,320},{448,384},... | collective-permute-start | bytes 9224 | tf_op jit(solution)/shard_map/while/body/eval_jaxpr/ppermute | solution.py:18
  257.9 6.8 %collective-permute-start.9 = (f32[2,2,4,16,3]{4,2,1,3,0:T(4,128)S(1)}, f32[2,2,4,16,3]{4,2,1,3,0:T(4,128)S(1)}, u32[]{:S(2)}, u32[]{:S(2)}) collective-permute-start(f32[2,2,4,16,3]{4,2,1,3,0:T(4,128)S(1)} %get-tuple-element.288), channel_id=1, source_target_pairs={{0,64},{64,128},{128,192},{192,256},{256,320},{320,384},{384,448},... | collective-permute-start | bytes 9224 | tf_op jit(solution)/shard_map/while/body/eval_jaxpr/ppermute | solution.py:17
  266.8 8.1 %collective-permute-start.11 = (f32[2,2,4,3,134]{4,2,1,3,0:T(4,128)S(1)}, f32[2,2,4,3,134]{4,2,1,3,0:T(4,128)S(1)}, u32[]{:S(2)}, u32[]{:S(2)}) collective-permute-start(f32[2,2,4,3,134]{4,2,1,3,0:T(4,128)S(1)} %get-tuple-element.290), channel_id=1, source_target_pairs={{0,1},{1,2},{2,3},{3,4},{4,5},{5,6},{6,7},{7,8},{8,9},{9,10},{10,1... | collective-permute-start | bytes 77192 | tf_op jit(solution)/shard_map/while/body/eval_jaxpr/ppermute | solution.py:17
  280.2 8.5 %collective-permute-start = (f32[1,2,4,16,3]{4,2,1,3,0:T(4,128)S(1)}, f32[1,2,4,16,3]{4,2,1,3,0:T(4,128)S(1)}, u32[]{:S(2)}, u32[]{:S(2)}) collective-permute-start(f32[1,2,4,16,3]{4,2,1,3,0:T(4,128)S(1)} %get-tuple-element.277), channel_id=1, source_target_pairs={{64,0},{128,64},{192,128},{256,192},{320,256},{384,320},{448,384},... | collective-permute-start | bytes 4616 | tf_op jit(solution)/shard_map/while/body/eval_jaxpr/ppermute | solution.py:18
  281.5 7.2 %collective-permute-start.1 = (f32[1,2,4,16,3]{4,2,1,3,0:T(4,128)S(1)}, f32[1,2,4,16,3]{4,2,1,3,0:T(4,128)S(1)}, u32[]{:S(2)}, u32[]{:S(2)}) collective-permute-start(f32[1,2,4,16,3]{4,2,1,3,0:T(4,128)S(1)} %get-tuple-element.278), channel_id=1, source_target_pairs={{0,64},{64,128},{128,192},{192,256},{256,320},{320,384},{384,448},... | collective-permute-start | bytes 4616 | tf_op jit(solution)/shard_map/while/body/eval_jaxpr/ppermute | solution.py:17
  290.7 7.8 %collective-permute-start.3 = (f32[1,2,4,3,134]{4,2,1,3,0:T(4,128)S(1)}, f32[1,2,4,3,134]{4,2,1,3,0:T(4,128)S(1)}, u32[]{:S(2)}, u32[]{:S(2)}) collective-permute-start(f32[1,2,4,3,134]{4,2,1,3,0:T(4,128)S(1)} %get-tuple-element.280), channel_id=1, source_target_pairs={{0,1},{1,2},{2,3},{3,4},{4,5},{5,6},{6,7},{7,8},{8,9},{9,10},{10,1... | collective-permute-start | bytes 38600 | tf_op jit(solution)/shard_map/while/body/eval_jaxpr/ppermute | solution.py:17
  301.5 6.5 %collective-permute-start.4 = (f32[2,2,4,16,3]{4,2,1,3,0:T(4,128)S(1)}, f32[2,2,4,16,3]{4,2,1,3,0:T(4,128)S(1)}, u32[]{:S(2)}, u32[]{:S(2)}) collective-permute-start(f32[2,2,4,16,3]{4,2,1,3,0:T(4,128)S(1)} %get-tuple-element.283), channel_id=1, source_target_pairs={{64,0},{128,64},{192,128},{256,192},{320,256},{384,320},{448,384},... | collective-permute-start | bytes 9224 | tf_op jit(solution)/shard_map/while/body/eval_jaxpr/ppermute | solution.py:18
  310.9 8.1 %collective-permute-start.7 = (f32[2,2,4,3,134]{4,2,1,3,0:T(4,128)S(1)}, f32[2,2,4,3,134]{4,2,1,3,0:T(4,128)S(1)}, u32[]{:S(2)}, u32[]{:S(2)}) collective-permute-start(f32[2,2,4,3,134]{4,2,1,3,0:T(4,128)S(1)} %get-tuple-element.286), channel_id=1, source_target_pairs={{0,1},{1,2},{2,3},{3,4},{4,5},{5,6},{6,7},{7,8},{8,9},{9,10},{10,1... | collective-permute-start | bytes 77192 | tf_op jit(solution)/shard_map/while/body/eval_jaxpr/ppermute | solution.py:17
  321.4 7.4 %collective-permute-start.8 = (f32[2,2,4,16,3]{4,2,1,3,0:T(4,128)S(1)}, f32[2,2,4,16,3]{4,2,1,3,0:T(4,128)S(1)}, u32[]{:S(2)}, u32[]{:S(2)}) collective-permute-start(f32[2,2,4,16,3]{4,2,1,3,0:T(4,128)S(1)} %get-tuple-element.287), channel_id=1, source_target_pairs={{64,0},{128,64},{192,128},{256,192},{320,256},{384,320},{448,384},... | collective-permute-start | bytes 9224 | tf_op jit(solution)/shard_map/while/body/eval_jaxpr/ppermute | solution.py:18
  322.7 6.8 %collective-permute-start.9 = (f32[2,2,4,16,3]{4,2,1,3,0:T(4,128)S(1)}, f32[2,2,4,16,3]{4,2,1,3,0:T(4,128)S(1)}, u32[]{:S(2)}, u32[]{:S(2)}) collective-permute-start(f32[2,2,4,16,3]{4,2,1,3,0:T(4,128)S(1)} %get-tuple-element.288), channel_id=1, source_target_pairs={{0,64},{64,128},{128,192},{192,256},{256,320},{320,384},{384,448},... | collective-permute-start | bytes 9224 | tf_op jit(solution)/shard_map/while/body/eval_jaxpr/ppermute | solution.py:17
  331.6 8.1 %collective-permute-start.11 = (f32[2,2,4,3,134]{4,2,1,3,0:T(4,128)S(1)}, f32[2,2,4,3,134]{4,2,1,3,0:T(4,128)S(1)}, u32[]{:S(2)}, u32[]{:S(2)}) collective-permute-start(f32[2,2,4,3,134]{4,2,1,3,0:T(4,128)S(1)} %get-tuple-element.290), channel_id=1, source_target_pairs={{0,1},{1,2},{2,3},{3,4},{4,5},{5,6},{6,7},{7,8},{8,9},{9,10},{10,1... | collective-permute-start | bytes 77192 | tf_op jit(solution)/shard_map/while/body/eval_jaxpr/ppermute | solution.py:17
  345.0 8.5 %collective-permute-start = (f32[1,2,4,16,3]{4,2,1,3,0:T(4,128)S(1)}, f32[1,2,4,16,3]{4,2,1,3,0:T(4,128)S(1)}, u32[]{:S(2)}, u32[]{:S(2)}) collective-permute-start(f32[1,2,4,16,3]{4,2,1,3,0:T(4,128)S(1)} %get-tuple-element.277), channel_id=1, source_target_pairs={{64,0},{128,64},{192,128},{256,192},{320,256},{384,320},{448,384},... | collective-permute-start | bytes 4616 | tf_op jit(solution)/shard_map/while/body/eval_jaxpr/ppermute | solution.py:18
  346.3 7.2 %collective-permute-start.1 = (f32[1,2,4,16,3]{4,2,1,3,0:T(4,128)S(1)}, f32[1,2,4,16,3]{4,2,1,3,0:T(4,128)S(1)}, u32[]{:S(2)}, u32[]{:S(2)}) collective-permute-start(f32[1,2,4,16,3]{4,2,1,3,0:T(4,128)S(1)} %get-tuple-element.278), channel_id=1, source_target_pairs={{0,64},{64,128},{128,192},{192,256},{256,320},{320,384},{384,448},... | collective-permute-start | bytes 4616 | tf_op jit(solution)/shard_map/while/body/eval_jaxpr/ppermute | solution.py:17
  355.5 7.8 %collective-permute-start.3 = (f32[1,2,4,3,134]{4,2,1,3,0:T(4,128)S(1)}, f32[1,2,4,3,134]{4,2,1,3,0:T(4,128)S(1)}, u32[]{:S(2)}, u32[]{:S(2)}) collective-permute-start(f32[1,2,4,3,134]{4,2,1,3,0:T(4,128)S(1)} %get-tuple-element.280), channel_id=1, source_target_pairs={{0,1},{1,2},{2,3},{3,4},{4,5},{5,6},{6,7},{7,8},{8,9},{9,10},{10,1... | collective-permute-start | bytes 38600 | tf_op jit(solution)/shard_map/while/body/eval_jaxpr/ppermute | solution.py:17
  366.3 6.5 %collective-permute-start.4 = (f32[2,2,4,16,3]{4,2,1,3,0:T(4,128)S(1)}, f32[2,2,4,16,3]{4,2,1,3,0:T(4,128)S(1)}, u32[]{:S(2)}, u32[]{:S(2)}) collective-permute-start(f32[2,2,4,16,3]{4,2,1,3,0:T(4,128)S(1)} %get-tuple-element.283), channel_id=1, source_target_pairs={{64,0},{128,64},{192,128},{256,192},{320,256},{384,320},{448,384},... | collective-permute-start | bytes 9224 | tf_op jit(solution)/shard_map/while/body/eval_jaxpr/ppermute | solution.py:18
  375.6 8.1 %collective-permute-start.7 = (f32[2,2,4,3,134]{4,2,1,3,0:T(4,128)S(1)}, f32[2,2,4,3,134]{4,2,1,3,0:T(4,128)S(1)}, u32[]{:S(2)}, u32[]{:S(2)}) collective-permute-start(f32[2,2,4,3,134]{4,2,1,3,0:T(4,128)S(1)} %get-tuple-element.286), channel_id=1, source_target_pairs={{0,1},{1,2},{2,3},{3,4},{4,5},{5,6},{6,7},{7,8},{8,9},{9,10},{10,1... | collective-permute-start | bytes 77192 | tf_op jit(solution)/shard_map/while/body/eval_jaxpr/ppermute | solution.py:17
  386.2 7.4 %collective-permute-start.8 = (f32[2,2,4,16,3]{4,2,1,3,0:T(4,128)S(1)}, f32[2,2,4,16,3]{4,2,1,3,0:T(4,128)S(1)}, u32[]{:S(2)}, u32[]{:S(2)}) collective-permute-start(f32[2,2,4,16,3]{4,2,1,3,0:T(4,128)S(1)} %get-tuple-element.287), channel_id=1, source_target_pairs={{64,0},{128,64},{192,128},{256,192},{320,256},{384,320},{448,384},... | collective-permute-start | bytes 9224 | tf_op jit(solution)/shard_map/while/body/eval_jaxpr/ppermute | solution.py:18
  387.5 6.8 %collective-permute-start.9 = (f32[2,2,4,16,3]{4,2,1,3,0:T(4,128)S(1)}, f32[2,2,4,16,3]{4,2,1,3,0:T(4,128)S(1)}, u32[]{:S(2)}, u32[]{:S(2)}) collective-permute-start(f32[2,2,4,16,3]{4,2,1,3,0:T(4,128)S(1)} %get-tuple-element.288), channel_id=1, source_target_pairs={{0,64},{64,128},{128,192},{192,256},{256,320},{320,384},{384,448},... | collective-permute-start | bytes 9224 | tf_op jit(solution)/shard_map/while/body/eval_jaxpr/ppermute | solution.py:17
  396.4 8.1 %collective-permute-start.11 = (f32[2,2,4,3,134]{4,2,1,3,0:T(4,128)S(1)}, f32[2,2,4,3,134]{4,2,1,3,0:T(4,128)S(1)}, u32[]{:S(2)}, u32[]{:S(2)}) collective-permute-start(f32[2,2,4,3,134]{4,2,1,3,0:T(4,128)S(1)} %get-tuple-element.290), channel_id=1, source_target_pairs={{0,1},{1,2},{2,3},{3,4},{4,5},{5,6},{6,7},{7,8},{8,9},{9,10},{10,1... | collective-permute-start | bytes 77192 | tf_op jit(solution)/shard_map/while/body/eval_jaxpr/ppermute | solution.py:17
  409.7 8.5 %collective-permute-start = (f32[1,2,4,16,3]{4,2,1,3,0:T(4,128)S(1)}, f32[1,2,4,16,3]{4,2,1,3,0:T(4,128)S(1)}, u32[]{:S(2)}, u32[]{:S(2)}) collective-permute-start(f32[1,2,4,16,3]{4,2,1,3,0:T(4,128)S(1)} %get-tuple-element.277), channel_id=1, source_target_pairs={{64,0},{128,64},{192,128},{256,192},{320,256},{384,320},{448,384},... | collective-permute-start | bytes 4616 | tf_op jit(solution)/shard_map/while/body/eval_jaxpr/ppermute | solution.py:18
  411.0 7.2 %collective-permute-start.1 = (f32[1,2,4,16,3]{4,2,1,3,0:T(4,128)S(1)}, f32[1,2,4,16,3]{4,2,1,3,0:T(4,128)S(1)}, u32[]{:S(2)}, u32[]{:S(2)}) collective-permute-start(f32[1,2,4,16,3]{4,2,1,3,0:T(4,128)S(1)} %get-tuple-element.278), channel_id=1, source_target_pairs={{0,64},{64,128},{128,192},{192,256},{256,320},{320,384},{384,448},... | collective-permute-start | bytes 4616 | tf_op jit(solution)/shard_map/while/body/eval_jaxpr/ppermute | solution.py:17
  420.3 7.8 %collective-permute-start.3 = (f32[1,2,4,3,134]{4,2,1,3,0:T(4,128)S(1)}, f32[1,2,4,3,134]{4,2,1,3,0:T(4,128)S(1)}, u32[]{:S(2)}, u32[]{:S(2)}) collective-permute-start(f32[1,2,4,3,134]{4,2,1,3,0:T(4,128)S(1)} %get-tuple-element.280), channel_id=1, source_target_pairs={{0,1},{1,2},{2,3},{3,4},{4,5},{5,6},{6,7},{7,8},{8,9},{9,10},{10,1... | collective-permute-start | bytes 38600 | tf_op jit(solution)/shard_map/while/body/eval_jaxpr/ppermute | solution.py:17
  431.1 6.5 %collective-permute-start.4 = (f32[2,2,4,16,3]{4,2,1,3,0:T(4,128)S(1)}, f32[2,2,4,16,3]{4,2,1,3,0:T(4,128)S(1)}, u32[]{:S(2)}, u32[]{:S(2)}) collective-permute-start(f32[2,2,4,16,3]{4,2,1,3,0:T(4,128)S(1)} %get-tuple-element.283), channel_id=1, source_target_pairs={{64,0},{128,64},{192,128},{256,192},{320,256},{384,320},{448,384},... | collective-permute-start | bytes 9224 | tf_op jit(solution)/shard_map/while/body/eval_jaxpr/ppermute | solution.py:18
  440.4 8.1 %collective-permute-start.7 = (f32[2,2,4,3,134]{4,2,1,3,0:T(4,128)S(1)}, f32[2,2,4,3,134]{4,2,1,3,0:T(4,128)S(1)}, u32[]{:S(2)}, u32[]{:S(2)}) collective-permute-start(f32[2,2,4,3,134]{4,2,1,3,0:T(4,128)S(1)} %get-tuple-element.286), channel_id=1, source_target_pairs={{0,1},{1,2},{2,3},{3,4},{4,5},{5,6},{6,7},{7,8},{8,9},{9,10},{10,1... | collective-permute-start | bytes 77192 | tf_op jit(solution)/shard_map/while/body/eval_jaxpr/ppermute | solution.py:17
  451.0 7.4 %collective-permute-start.8 = (f32[2,2,4,16,3]{4,2,1,3,0:T(4,128)S(1)}, f32[2,2,4,16,3]{4,2,1,3,0:T(4,128)S(1)}, u32[]{:S(2)}, u32[]{:S(2)}) collective-permute-start(f32[2,2,4,16,3]{4,2,1,3,0:T(4,128)S(1)} %get-tuple-element.287), channel_id=1, source_target_pairs={{64,0},{128,64},{192,128},{256,192},{320,256},{384,320},{448,384},... | collective-permute-start | bytes 9224 | tf_op jit(solution)/shard_map/while/body/eval_jaxpr/ppermute | solution.py:18
  452.3 6.8 %collective-permute-start.9 = (f32[2,2,4,16,3]{4,2,1,3,0:T(4,128)S(1)}, f32[2,2,4,16,3]{4,2,1,3,0:T(4,128)S(1)}, u32[]{:S(2)}, u32[]{:S(2)}) collective-permute-start(f32[2,2,4,16,3]{4,2,1,3,0:T(4,128)S(1)} %get-tuple-element.288), channel_id=1, source_target_pairs={{0,64},{64,128},{128,192},{192,256},{256,320},{320,384},{384,448},... | collective-permute-start | bytes 9224 | tf_op jit(solution)/shard_map/while/body/eval_jaxpr/ppermute | solution.py:17
  461.2 8.1 %collective-permute-start.11 = (f32[2,2,4,3,134]{4,2,1,3,0:T(4,128)S(1)}, f32[2,2,4,3,134]{4,2,1,3,0:T(4,128)S(1)}, u32[]{:S(2)}, u32[]{:S(2)}) collective-permute-start(f32[2,2,4,3,134]{4,2,1,3,0:T(4,128)S(1)} %get-tuple-element.290), channel_id=1, source_target_pairs={{0,1},{1,2},{2,3},{3,4},{4,5},{5,6},{6,7},{7,8},{8,9},{9,10},{10,1... | collective-permute-start | bytes 77192 | tf_op jit(solution)/shard_map/while/body/eval_jaxpr/ppermute | solution.py:17
  474.5 8.5 %collective-permute-start = (f32[1,2,4,16,3]{4,2,1,3,0:T(4,128)S(1)}, f32[1,2,4,16,3]{4,2,1,3,0:T(4,128)S(1)}, u32[]{:S(2)}, u32[]{:S(2)}) collective-permute-start(f32[1,2,4,16,3]{4,2,1,3,0:T(4,128)S(1)} %get-tuple-element.277), channel_id=1, source_target_pairs={{64,0},{128,64},{192,128},{256,192},{320,256},{384,320},{448,384},... | collective-permute-start | bytes 4616 | tf_op jit(solution)/shard_map/while/body/eval_jaxpr/ppermute | solution.py:18
  475.8 7.2 %collective-permute-start.1 = (f32[1,2,4,16,3]{4,2,1,3,0:T(4,128)S(1)}, f32[1,2,4,16,3]{4,2,1,3,0:T(4,128)S(1)}, u32[]{:S(2)}, u32[]{:S(2)}) collective-permute-start(f32[1,2,4,16,3]{4,2,1,3,0:T(4,128)S(1)} %get-tuple-element.278), channel_id=1, source_target_pairs={{0,64},{64,128},{128,192},{192,256},{256,320},{320,384},{384,448},... | collective-permute-start | bytes 4616 | tf_op jit(solution)/shard_map/while/body/eval_jaxpr/ppermute | solution.py:17
  485.1 7.8 %collective-permute-start.3 = (f32[1,2,4,3,134]{4,2,1,3,0:T(4,128)S(1)}, f32[1,2,4,3,134]{4,2,1,3,0:T(4,128)S(1)}, u32[]{:S(2)}, u32[]{:S(2)}) collective-permute-start(f32[1,2,4,3,134]{4,2,1,3,0:T(4,128)S(1)} %get-tuple-element.280), channel_id=1, source_target_pairs={{0,1},{1,2},{2,3},{3,4},{4,5},{5,6},{6,7},{7,8},{8,9},{9,10},{10,1... | collective-permute-start | bytes 38600 | tf_op jit(solution)/shard_map/while/body/eval_jaxpr/ppermute | solution.py:17
  495.9 6.5 %collective-permute-start.4 = (f32[2,2,4,16,3]{4,2,1,3,0:T(4,128)S(1)}, f32[2,2,4,16,3]{4,2,1,3,0:T(4,128)S(1)}, u32[]{:S(2)}, u32[]{:S(2)}) collective-permute-start(f32[2,2,4,16,3]{4,2,1,3,0:T(4,128)S(1)} %get-tuple-element.283), channel_id=1, source_target_pairs={{64,0},{128,64},{192,128},{256,192},{320,256},{384,320},{448,384},... | collective-permute-start | bytes 9224 | tf_op jit(solution)/shard_map/while/body/eval_jaxpr/ppermute | solution.py:18
  505.2 8.1 %collective-permute-start.7 = (f32[2,2,4,3,134]{4,2,1,3,0:T(4,128)S(1)}, f32[2,2,4,3,134]{4,2,1,3,0:T(4,128)S(1)}, u32[]{:S(2)}, u32[]{:S(2)}) collective-permute-start(f32[2,2,4,3,134]{4,2,1,3,0:T(4,128)S(1)} %get-tuple-element.286), channel_id=1, source_target_pairs={{0,1},{1,2},{2,3},{3,4},{4,5},{5,6},{6,7},{7,8},{8,9},{9,10},{10,1... | collective-permute-start | bytes 77192 | tf_op jit(solution)/shard_map/while/body/eval_jaxpr/ppermute | solution.py:17
  515.8 7.4 %collective-permute-start.8 = (f32[2,2,4,16,3]{4,2,1,3,0:T(4,128)S(1)}, f32[2,2,4,16,3]{4,2,1,3,0:T(4,128)S(1)}, u32[]{:S(2)}, u32[]{:S(2)}) collective-permute-start(f32[2,2,4,16,3]{4,2,1,3,0:T(4,128)S(1)} %get-tuple-element.287), channel_id=1, source_target_pairs={{64,0},{128,64},{192,128},{256,192},{320,256},{384,320},{448,384},... | collective-permute-start | bytes 9224 | tf_op jit(solution)/shard_map/while/body/eval_jaxpr/ppermute | solution.py:18
  517.1 6.8 %collective-permute-start.9 = (f32[2,2,4,16,3]{4,2,1,3,0:T(4,128)S(1)}, f32[2,2,4,16,3]{4,2,1,3,0:T(4,128)S(1)}, u32[]{:S(2)}, u32[]{:S(2)}) collective-permute-start(f32[2,2,4,16,3]{4,2,1,3,0:T(4,128)S(1)} %get-tuple-element.288), channel_id=1, source_target_pairs={{0,64},{64,128},{128,192},{192,256},{256,320},{320,384},{384,448},... | collective-permute-start | bytes 9224 | tf_op jit(solution)/shard_map/while/body/eval_jaxpr/ppermute | solution.py:17
  526.0 8.1 %collective-permute-start.11 = (f32[2,2,4,3,134]{4,2,1,3,0:T(4,128)S(1)}, f32[2,2,4,3,134]{4,2,1,3,0:T(4,128)S(1)}, u32[]{:S(2)}, u32[]{:S(2)}) collective-permute-start(f32[2,2,4,3,134]{4,2,1,3,0:T(4,128)S(1)} %get-tuple-element.290), channel_id=1, source_target_pairs={{0,1},{1,2},{2,3},{3,4},{4,5},{5,6},{6,7},{7,8},{8,9},{9,10},{10,1... | collective-permute-start | bytes 77192 | tf_op jit(solution)/shard_map/while/body/eval_jaxpr/ppermute | solution.py:17
  (35 other events, 202.4 us)
where the time goes:
time: 557 us; the launch traced here: 554 us
  starting transfers between devices  312 us (56%)
  waiting for transfers between devices  113 us (20%)
  other arithmetic  86.8 us (16%)
  matrix products  15.4 us (3%)
  blocking collectives  14.2 us (3%)
  local copies, waits for them, and re-layouts  8.81 us (2%)
    ppermute x48, starting transfers between devices, extended(): before = lax.ppermute(last, axis, up)  221 us
    ppermute x48, waiting for transfers between devices, extended(): before = lax.ppermute(last, axis, up)  108 us
    ppermute x48, starting transfers between devices, extended(): after = lax.ppermute(initial, axis, down)  86.8 us
    select_n x72, other arithmetic, clip_domain(): return jnp.where(keep, field, 0.0)  49.1 us
    dot_general x80, matrix products, coefficients(): jnp.einsum('cij,fcp->fpij', onehot, table_part[:, :, :, degree], precisio...  15.4 us
    all_to_all x1, blocking collectives, body(): lax.all_to_all(image, 'depth', split_axis=0, concat_axis=2, tiled=True)  14.2 us
  transfers between devices with their start and end apart: 97, of which 41 were waited for; matrix products, arithmetic and copies ran while one was open for 3% of the time, Pallas kernels for 0%

commit v1 on v0

v1 whole, which is shorter than its diff:
```python
import functools

import jax
import jax.numpy as jnp
from jax import lax
from jax.experimental import pallas as pl
from jax.experimental.pallas import tpu as pltpu
from jax.sharding import PartitionSpec as P

PASSES = 9
CLASSES = 8
FIELDS = 8
LANES = 128
FUSED = 3
LAG = 2
UNROLL = 8
PHASES = (2, 3, 3)
TILE_ROWS = 32
TILE_COLS = 64
WIDE = 256
ORIGIN = (WIDE - TILE_COLS) // 2
PAD = 2


def lane_ids():
    return lax.broadcasted_iota(jnp.int32, (FIELDS, LANES), 1)


def inside(first_col, col_limit):
    cols = lane_ids() + first_col
    return jnp.where((cols >= 0) & (cols < col_limit), 0.25, 0.0).astype(jnp.float32)


def blurred(parts, lane):
    ahead = [pltpu.roll(x, LANES - 1, 1) for x in parts]
    if len(parts) == 2:
        ahead = [jnp.where(lane == LANES - 1, ahead[1], ahead[0]), ahead[1]]
    pair = [x + y for x, y in zip(parts, ahead)]
    behind = [pltpu.roll(x, 1, 1) for x in pair]
    if len(parts) == 2:
        behind = [behind[0], jnp.where(lane == 0, behind[0], behind[1])]
    return [x + y for x, y in zip(pair, behind)]


def swapped(x, sub):
    up = pltpu.roll(x, FIELDS - 1, 0)
    down = pltpu.roll(x, 1, 0)
    return jnp.where(sub % 2 == 0, up, down)


def sweep(first_degree, low, high, tiles, refs, tabs, scale):
    cur, summed, acc, crs, idx = refs
    lane = lane_ids()
    sub = lax.broadcasted_iota(jnp.int32, (FIELDS, LANES), 0)
    opening = first_degree == 0
    closing = first_degree + FUSED == PASSES
    span = range(tiles)

    def row(ref, at):
        return [ref[at, :, t * LANES : (t + 1) * LANES] for t in span]

    def put(ref, at, parts):
        for t in span:
            ref[at, :, t * LANES : (t + 1) * LANES] = parts[t]

    def step(base, offset, live, valid=None):
        at = base + offset
        live[("t", 0, offset + 1)] = row(cur, at + 1)
        for level in range(FUSED, 0, -1) if LAG > 1 else range(1, FUSED + 1):
            own = offset - (level - 1) * LAG
            if valid is not None and own < valid + level:
                if level == 1 or own >= valid + level - 1:
                    pass
                continue
            here = live[("t", level - 1, own)]
            after = live[("t", level - 1, own + 1)]
            pair = [x + y for x, y in zip(here, after)]
            both = [x + y for x, y in zip(live[("u", level - 1, own - 1)], pair)]
            live[("u", level - 1, own)] = pair
            both = blurred(both, lane)
            if opening and level == 1:
                total = [(0.5 * s) * x for s, x in zip(scale, both)]
            else:
                before = row(summed, at) if level == 1 else live[("e", level - 1, own)]
                total = [s * x - e for s, x, e in zip(scale, both, before)]
            live[("e", level, own)] = total
            live[("t", level, own)] = [e - x for e, x in zip(total, here)]
        done = offset - (FUSED - 1) * LAG
        if valid is not None and done < valid + FUSED:
            return
        place = base + done
        picks = row(idx, place)
        levels = list(range(0 if opening else 1, FUSED + 1))
        terms = [row(cur, place) if level == 0 else live[("t", level, done)] for level in levels]
        new_acc = [None] * tiles if opening else row(acc, place)
        new_crs = [None] * tiles if opening else row(crs, place)
        for level, term in zip(levels, terms):
            real_tab, imag_tab = tabs(first_degree + level)
            for t in span:
                real = jnp.take_along_axis(real_tab, picks[t], axis=1) * term[t]
                imag = jnp.take_along_axis(imag_tab, picks[t], axis=1) * term[t]
                new_acc[t] = real if new_acc[t] is None else new_acc[t] + real
                new_crs[t] = imag if new_crs[t] is None else new_crs[t] + imag
        if closing:
            put(cur, place, [x + swapped(y, sub) for x, y in zip(new_acc, new_crs)])
        else:
            put(acc, place, new_acc)
            put(crs, place, new_crs)
            put(cur, place, live[("t", FUSED, done)])
            put(summed, place, live[("e", FUSED, done)])

    def seed(live, valid, offset):
        for level in range(1, FUSED):
            edge = valid + level
            one, two = ("t", level, edge), ("t", level, edge + 1)
            if one in live and two in live and ("u", level, edge) not in live:
                live[("u", level, edge)] = [x + y for x, y in zip(live[one], live[two])]

    def keys(offset):
        out = [("t", 0, offset), ("u", 0, offset - 1)]
        for level in range(1, FUSED):
            newest = offset - 1 - (level - 1) * LAG
            for r in range(offset - (FUSED - 1) * LAG, newest + 1):
                out.append(("t", level, r))
            for r in range(offset - level * LAG, newest + 1):
                out.append(("e", level, r))
            out.append(("u", level, offset - level * LAG - 1))
        return out

    start = FUSED + (FUSED - 1) * LAG
    live = {("t", 0, 0): row(cur, low), ("t", 0, 1): row(cur, low + 1)}
    live[("u", 0, 0)] = [x + y for x, y in zip(live[("t", 0, 0)], live[("t", 0, 1)])]
    for offset in range(1, start):
        step(low, offset, live, valid=0)
        seed(live, 0, offset)
    count = high - low - 2 * FUSED
    carry = [live[key] for key in keys(start)]

    def block(base, carry, length):
        live = dict(zip(keys(0), carry))
        for offset in range(length):
            step(base, offset, live)
        return [live[key] for key in keys(length)]

    def body(i, carry):
        return block(low + start + i * UNROLL, carry, UNROLL)

    whole = count // UNROLL
    carry = lax.fori_loop(0, whole, body, carry)
    if count % UNROLL:
        block(low + start + whole * UNROLL, carry, count % UNROLL)


def centred(parts, lane):
    if len(parts) == 1:
        return parts[0]
    left, right = (pltpu.roll(x, LANES // 2, 1) for x in parts)
    return jnp.where(lane < LANES // 2, left, right)


def run_phase(steps, first_depth, tiles, flags, cur, refs, classes, tab_ref, image_ref, scale):
    halo = steps * PASSES
    lane = lane_ids()
    sub = lax.broadcasted_iota(jnp.int32, (FIELDS, LANES), 0)
    summed, acc, crs, idx = refs
    total = TILE_ROWS + 2 * halo

    @pl.when(flags[0] == 1)
    def _():
        cur[halo - 1] = jnp.zeros_like(cur[0])
        for i in range(1, halo):
            cur[halo - 1 - i] = -cur[halo - 1 + i]

    @pl.when(flags[1] == 1)
    def _():
        end = halo + TILE_ROWS
        cur[end] = jnp.zeros_like(cur[0])
        for i in range(1, halo):
            cur[end + i] = -cur[end - i]

    def tabs(degree):
        return tab_ref[degree, 0], tab_ref[degree, 1]

    for local in range(steps):
        reach = (steps - 1 - local) * PASSES
        above, own, below = classes(first_depth + local)
        depth = first_depth + local

        def spread(to, one):
            idx[to] = jnp.broadcast_to(one, idx.shape[1:]).astype(jnp.int32)

        if reach:
            for i in range(reach):
                spread(halo - reach + i, above(i, reach))
                spread(halo + TILE_ROWS + i, below(i, reach))
        for i in range(TILE_ROWS):
            spread(halo + i, own(i))
        if reach:
            @pl.when(flags[0] == 1)
            def _():
                for i in range(1, reach):
                    idx[halo - 1 - i] = idx[halo - 1 + i]

            @pl.when(flags[1] == 1)
            def _():
                end = halo + TILE_ROWS
                for i in range(1, reach):
                    idx[end + i] = idx[end - i]

        low, high = local * PASSES, total - local * PASSES
        for part in range(PASSES // FUSED):
            sweep(
                part * FUSED,
                low + part * FUSED,
                high - part * FUSED,
                tiles,
                (cur, summed, acc, crs, idx),
                tabs,
                scale,
            )

        def pictured(i, _):
            parts = [cur[halo + i, :, t * LANES : (t + 1) * LANES] for t in range(tiles)]
            field = centred(parts, lane)
            product = field * pltpu.roll(field, FIELDS - 2, 0)
            product = jnp.where(sub % 4 < 2, product, 0.0)
            image_ref[local, pl.ds(i, 1), :] = jnp.sum(product, axis=0, keepdims=True)
            return 0

        lax.fori_loop(0, TILE_ROWS, pictured, 0, unroll=4)


def class_slots():
    slots = []
    depth = 0
    for steps in PHASES:
        for local in range(steps):
            for first in range(0, (steps - 1 - local) * PASSES, PASSES):
                slots.append((depth, first))
            depth += 1
    return slots


def slot_of(depth, first):
    return class_slots().index((depth, first))


def scatter_kernel(part_ref, surface_ref, velocity_ref, out_ref, wide_ref):
    del part_ref
    columns = surface_ref.shape[-1]
    count = out_ref.shape[0]
    strip_rows = surface_ref.shape[-2]
    wide_ref[...] = jnp.zeros_like(wide_ref)
    wide_ref[0:strip_rows, LANES : LANES + columns] = surface_ref[0]
    wide_ref[strip_rows:, LANES : LANES + columns] = velocity_ref[0].astype(jnp.float32)
    for c in range(count):
        begin = LANES - ORIGIN + TILE_COLS * c
        out_ref[c] = wide_ref[:, begin : begin + WIDE]


def gather_kernel(in_ref, tile_ref, class_ref, up_ref, down_ref):
    strip_rows = in_ref.shape[1] // 2
    halo = PHASES[0] * PASSES
    for parity in range(2):
        for i in range(strip_rows):
            to = parity * strip_rows + i
            for d in range(FIELDS):
                tile_ref[to, d : d + 1, :] = in_ref[2 * d + parity, i : i + 1, :]
                class_ref[to, d : d + 1, :] = in_ref[
                    2 * d + parity, strip_rows + i : strip_rows + i + 1, :
                ]
    up_ref[0:halo] = tile_ref[0:halo]
    down_ref[0:halo] = tile_ref[TILE_ROWS - halo : TILE_ROWS]
    up_ref[halo:] = jnp.zeros_like(up_ref[halo:])
    down_ref[halo:] = jnp.zeros_like(down_ref[halo:])
    for slot, (depth, first) in enumerate(class_slots()):
        for i in range(PASSES):
            up_ref[halo + i, slot : slot + 1, :] = class_ref[first + i, depth : depth + 1, :]
            far = TILE_ROWS - PASSES - first + i
            down_ref[halo + i, slot : slot + 1, :] = class_ref[far, depth : depth + 1, :]


def class_rows(above_ref, own_ref, below_ref, base, lanes):
    def reader(depth):
        def above(i, reach):
            back = reach - 1 - i
            first = back // PASSES * PASSES
            slot = slot_of(depth, first)
            at = base + PASSES - 1 - (back - first)
            return above_ref[at, slot : slot + 1, lanes]

        def own(i):
            return own_ref[i, depth : depth + 1, lanes]

        def below(i, reach):
            first = i // PASSES * PASSES
            slot = slot_of(depth, first)
            return below_ref[base + i - first, slot : slot + 1, lanes]

        return above, own, below

    return reader


def phase_kernel(
    phase, col_limit, classes_narrow, scalars_ref, above_ref, tile_ref, below_ref, cls_above_ref,
    cls_ref, cls_below_ref, tab_ref, *rest
):
    steps = PHASES[phase]
    halo = steps * PASSES
    tiles = tile_ref.shape[-1] // LANES
    last = phase == len(PHASES) - 1
    if last:
        image_ref, cur, *refs = rest
    else:
        image_ref, out_ref, up_ref, down_ref, cur, *refs = rest
    cur[0:halo] = above_ref[0:halo]
    cur[halo : halo + TILE_ROWS] = tile_ref[...]
    cur[halo + TILE_ROWS : TILE_ROWS + 2 * halo] = below_ref[0:halo]
    first_col = scalars_ref[2] - (ORIGIN if tiles == 2 else ORIGIN - LANES // 2)
    scale = [inside(first_col + t * LANES, col_limit) for t in range(tiles)]
    reader = class_rows(
        cls_above_ref, cls_ref, cls_below_ref, PHASES[0] * PASSES if not classes_narrow else 0,
        slice(0, tiles * LANES),
    )
    run_phase(
        steps, sum(PHASES[:phase]), tiles, (scalars_ref[0], scalars_ref[1]), cur, refs, reader,
        tab_ref, image_ref, scale,
    )
    if last:
        return
    lane = lane_ids()
    out_tiles = out_ref.shape[-1] // LANES
    next_halo = PHASES[phase + 1] * PASSES

    def emit(i, _):
        parts = [cur[halo + i, :, t * LANES : (t + 1) * LANES] for t in range(tiles)]
        if out_tiles < tiles:
            parts = [centred(parts, lane)]
        for t in range(out_tiles):
            out_ref[i, :, t * LANES : (t + 1) * LANES] = parts[t]
        return 0

    lax.fori_loop(0, TILE_ROWS, emit, 0, unroll=4)
    up_ref[...] = out_ref[0:next_halo]
    down_ref[...] = out_ref[TILE_ROWS - next_halo : TILE_ROWS]


def narrow_kernel(above_ref, own_ref, below_ref, out_above, out_own, out_below):
    lane = lane_ids()
    base = PHASES[0] * PASSES
    for source, target, offset in (
        (above_ref, out_above, base), (own_ref, out_own, 0), (below_ref, out_below, base)
    ):
        for i in range(target.shape[0]):
            parts = [source[offset + i, :, t * LANES : (t + 1) * LANES] for t in range(2)]
            target[i] = centred(parts, lane)


def collect_kernel(in_ref, out_ref):
    lane = lax.broadcasted_iota(jnp.int32, (in_ref.shape[1], LANES), 1)
    shift = (LANES - TILE_COLS) // 2
    for t in range(out_ref.shape[-1] // LANES):
        left = pltpu.roll(in_ref[2 * t], LANES - shift, 1)
        right = pltpu.roll(in_ref[2 * t + 1], shift, 1)
        out_ref[0, :, t * LANES : (t + 1) * LANES] = jnp.where(lane < TILE_COLS, left, right)


def coefficient_tables(table):
    by_field = jnp.repeat(jnp.transpose(table, (3, 2, 0, 1)), 4, axis=2)
    signs = jnp.array([1.0, -1.0, -1.0, 1.0] * 2, jnp.float32)
    parts = jnp.stack([jnp.ones_like(signs), signs])
    by_field = by_field * parts[None, :, :, None]
    return jnp.pad(by_field, ((0, 0), (0, 0), (0, 0), (0, LANES - CLASSES)))


VMEM = pl.BlockSpec(memory_space=pltpu.VMEM)
SMEM = pl.BlockSpec(memory_space=pltpu.SMEM)


def shaped(*dims):
    return jax.ShapeDtypeStruct(dims, jnp.float32)


def call(kernel, out_shape, in_specs, scratch=(), name=None):
    outs = jax.tree.map(lambda _: VMEM, out_shape)
    return pl.pallas_call(
        kernel, out_shape=out_shape, in_specs=in_specs, out_specs=outs, scratch_shapes=scratch, name=name
    )


def body(surface, velocity_class, table):
    parts, strips = lax.axis_size("depth"), lax.axis_size("strip")
    part, strip = lax.axis_index("depth"), lax.axis_index("strip")
    strip_rows, columns = velocity_class.shape[1:]
    chunks = 2 * parts
    groups = [
        [p * strips + 2 * j + b for p in range(parts) for b in range(2)] for j in range(strips // 2)
    ]
    both_axes = ("depth", "strip")
    scalars = jnp.stack(
        [
            (strip < 2).astype(jnp.int32),
            (strip >= strips - 2).astype(jnp.int32),
            (2 * part + strip % 2).astype(jnp.int32) * TILE_COLS,
        ]
    )
    planes = surface.reshape((FIELDS, strip_rows, columns))
    outgoing = pl.pallas_call(
        scatter_kernel,
        out_shape=shaped(chunks, 2 * strip_rows, WIDE),
        grid_spec=pltpu.PrefetchScalarGridSpec(
            num_scalar_prefetch=1,
            grid=(1,),
            in_specs=[
                pl.BlockSpec((1, strip_rows, columns), lambda i, at: (at[0], 0, 0)),
                pl.BlockSpec((1, strip_rows, columns), lambda i, at: (0, 0, 0)),
            ],
            out_specs=pl.BlockSpec((chunks, 2 * strip_rows, WIDE), lambda i, at: (0, 0, 0)),
            scratch_shapes=[pltpu.VMEM((2 * strip_rows, columns + 3 * LANES), jnp.float32)],
        ),
        name="scatter",
    )(part.reshape((1,)), planes, velocity_class)
    incoming = lax.all_to_all(outgoing, both_axes, 0, 0, axis_index_groups=groups, tiled=True)
    tables = coefficient_tables(table)

    halos = [steps * PASSES for steps in PHASES]
    tile, classes, up, down = call(
        gather_kernel,
        (
            shaped(TILE_ROWS, FIELDS, WIDE),
            shaped(TILE_ROWS, FIELDS, WIDE),
            shaped(halos[0] + PASSES, FIELDS, WIDE),
            shaped(halos[0] + PASSES, FIELDS, WIDE),
        ),
        [VMEM],
        name="gather",
    )(incoming)
    ahead = [(s, s + 2) for s in range(strips - 2)]
    back = [(s + 2, s) for s in range(strips - 2)]

    images = []
    class_args = None
    for phase, steps in enumerate(PHASES):
        above = lax.ppermute(down, "strip", ahead)
        below = lax.ppermute(up, "strip", back)
        last = phase == len(PHASES) - 1
        width = LANES if last else WIDE
        if phase == 0:
            class_args = (above, classes, below)
            narrow_args = call(
                narrow_kernel,
                (
                    shaped(PASSES, FIELDS, LANES),
                    shaped(TILE_ROWS, FIELDS, LANES),
                    shaped(PASSES, FIELDS, LANES),
                ),
                [VMEM] * 3,
                name="narrow",
            )(*class_args)
        rows = TILE_ROWS + 2 * halos[phase]
        out_shape = [shaped(steps, TILE_ROWS, LANES)]
        if not last:
            next_width = LANES if phase + 1 == len(PHASES) - 1 else WIDE
            out_shape.append(shaped(TILE_ROWS, FIELDS, next_width))
            out_shape += [shaped(halos[phase + 1], FIELDS, next_width)] * 2
        scratch = [pltpu.VMEM((rows + PAD, FIELDS, width), jnp.float32)] * 4
        scratch.append(pltpu.VMEM((rows + PAD, FIELDS, width), jnp.int32))
        out = call(
            functools.partial(phase_kernel, phase, columns, last),
            tuple(out_shape),
            [SMEM] + [VMEM] * 7,
            scratch,
            name=f"phase{phase}",
        )(scalars, above, tile, below, *(narrow_args if last else class_args), tables)
        images.append(out[0])
        if not last:
            tile, up, down = out[1:]
    image = jnp.concatenate(images, axis=0)
    image = image.reshape((chunks, strip_rows, LANES))
    image = lax.all_to_all(image, both_axes, 0, 0, axis_index_groups=groups, tiled=True)
    return call(collect_kernel, shaped(1, strip_rows, columns), [VMEM], name="collect")(image)


def solution(mesh):
    in_specs = (P(None, None, "strip", None), P("depth", "strip", None), P())
    out_specs = P("depth", "strip", None)
    return jax.shard_map(body, mesh=mesh, in_specs=in_specs, out_specs=out_specs, check_vma=False)
```

time: 557 us -> 201 us (0.36)
  starting transfers between devices: 312 us -> 36.6 us
  Pallas kernels: 0 us -> 117 us
  other arithmetic: 86.8 us -> 1.53 us
  waiting for transfers between devices: 113 us -> 29.8 us
  matrix products: 15.4 us -> 0 us
    ppermute x96 -> x6, starting transfers between devices: 308 us -> 30.7 us  [the longest x3 16.3 us: body(): above = lax.ppermute(down, 'strip', ahead)]
    pallas_call x0 -> x7, Pallas kernels: none -> 117 us  [the longest x3 109 us: body(): call(functools.partial(phase_kernel, phase, columns, last), tuple(out_sha...]
    ppermute x96 -> x6, waiting for transfers between devices: 108 us -> 20 us  [the longest x3 15 us: body(): below = lax.ppermute(up, 'strip', back)]
    select_n x72 -> x0, other arithmetic: 49.1 us -> none  [clip_domain(): return jnp.where(keep, field, 0.0)]
    add x40 -> x0, other arithmetic: 22.8 us -> none  [the longest x8 5.76 us: weigh(): result[:, 3] + (real_part * field[:, 3] - imag_part * field[:, 2])]
    dot_general x80 -> x0, matrix products: 15.4 us -> none  [coefficients(): jnp.einsum('cij,fcp->fpij', onehot, table_part[:, :, :, degree], precisio...]
  transfers between devices with their start and end apart: 97 -> 7, of which waited for: 41 -> 6; matrix products, arithmetic and copies ran while one was open for 3% -> 1% of each run, Pallas kernels for 0% -> 1%
where the time goes in v1:
time: 201 us; the launch traced here: 199 us
  Pallas kernels  117 us (58%)
  starting transfers between devices  36.6 us (18%)
  waiting for transfers between devices  29.8 us (15%)
  blocking collectives  9.81 us (5%)
  local copies, waits for them, and re-layouts  4.28 us (2%)
    pallas_call x3, Pallas kernels, body(): call(functools.partial(phase_kernel, phase, columns, last), tuple(out_sha...  109 us
    ppermute x3, starting transfers between devices, body(): above = lax.ppermute(down, 'strip', ahead)  16.3 us
    ppermute x3, waiting for transfers between devices, body(): below = lax.ppermute(up, 'strip', back)  15 us
    ppermute x3, starting transfers between devices, body(): below = lax.ppermute(up, 'strip', back)  14.4 us
    all_to_all x1, blocking collectives, body(): lax.all_to_all(image, both_axes, 0, 0, axis_index_groups=groups, tiled=True)  9.81 us
    all_to_all x1, waiting for transfers between devices, body(): lax.all_to_all(outgoing, both_axes, 0, 0, axis_index_groups=groups, tiled...  9.75 us
    all_to_all x1, starting transfers between devices, body(): lax.all_to_all(outgoing, both_axes, 0, 0, axis_index_groups=groups, tiled...  5.89 us
    ppermute x3, waiting for transfers between devices, body(): above = lax.ppermute(down, 'strip', ahead)  5.06 us
  transfers between devices with their start and end apart: 7, of which 6 were waited for; matrix products, arithmetic and copies ran while one was open for 1% of the time, Pallas kernels for 1%

profile of v1, /device:TPU:24, one launch (start us, length us, event | category | flops | bytes accessed | tf_op | source)
XLA Modules:
  0.0 199.3 jit_solution(11938330635556110564)
XLA Ops:
  0.0 1.9 scatter.1
  1.9 0.0 copy-start.9
  1.9 5.9 %all-to-all-start = ((f32[16,32,256]{2,1,0:T(8,128)}), f32[16,32,256]{2,1,0:T(8,128)S(1)}, u32[]{:S(2)}, u32[]{:S(2)}) async-start(f32[16,32,256]{2,1,0:T(8,128)} %scatter.1), calls=%async_computation | async-start | bytes 1048576 | tf_op jit(solution)/shard_map/all_to_all | solution.py:424
  7.8 0.0 copy-done.9
  7.8 0.1 copy.5
  8.0 9.8 %all-to-all-done.in_ref = f32[16,32,256]{2,1,0:T(8,128)S(1)} async-done(((f32[16,32,256]{2,1,0:T(8,128)}), f32[16,32,256]{2,1,0:T(8,128)S(1)}, u32[]{:S(2)}, u32[]{:S(2)}) %all-to-all-start) | async-done | bytes 524320 | tf_op jit(solution)/shard_map/all_to_all | solution.py:424
  17.7 0.0 copy-start.2
  17.7 0.8 copy-done.2
  18.5 2.2 %gather.1 = (f32[32,8,256]{2,1,0:T(8,128)}, f32[32,8,256]{2,1,0:T(8,128)}, f32[27,8,256]{2,1,0:T(8,128)}, f32[27,8,256]{2,1,0:T(8,128)}) custom-call(f32[16,32,256]{2,1,0:T(8,128)} %copy-done.2), custom_call_target="tpu_custom_call" | custom-call | tf_op jit(solution)/shard_map/gather/pallas_call | solution.py:428
  20.7 5.2 %collective-permute-start = (f32[27,8,256]{2,1,0:T(8,128)}, f32[27,8,256]{2,1,0:T(8,128)S(1)}, u32[]{:S(2)}, u32[]{:S(2)}) collective-permute-start(f32[27,8,256]{2,1,0:T(8,128)} %get-tuple-element.20), channel_id=1, source_target_pairs={{0,2},{1,3},{2,4},{3,5},{4,6},{5,7},{6,8},{7,9},{8,10},{9,11},{10,... | collective-permute-start | bytes 663560 | tf_op jit(solution)/shard_map/ppermute | solution.py:445
  25.9 7.9 %collective-permute-start.1 = (f32[27,8,256]{2,1,0:T(8,128)}, f32[27,8,256]{2,1,0:T(8,128)S(1)}, u32[]{:S(2)}, u32[]{:S(2)}) collective-permute-start(f32[27,8,256]{2,1,0:T(8,128)} %get-tuple-element.22), channel_id=1, source_target_pairs={{2,0},{3,1},{4,2},{5,3},{6,4},{7,5},{8,6},{9,7},{10,8},{11,9},{12,... | collective-permute-start | bytes 663560 | tf_op jit(solution)/shard_map/ppermute | solution.py:446
  33.8 0.0 copy-start.10
  33.8 0.7 copy-done.10
  34.5 0.1 broadcast_multiply_fusion
  34.6 0.6 pad.5.tab_ref
  35.2 0.6 pad_add_fusion.scalars_ref
  35.8 2.1 %collective-permute-done.above_ref.cls_above_ref = f32[27,8,256]{2,1,0:T(8,128)S(1)} collective-permute-done((f32[27,8,256]{2,1,0:T(8,128)}, f32[27,8,256]{2,1,0:T(8,128)S(1)}, u32[]{:S(2)}, u32[]{:S(2)}) %collective-permute-start) | collective-permute-done | bytes 221216 | tf_op jit(solution)/shard_map/ppermute | solution.py:445
  38.0 0.0 copy-start
  38.0 4.9 %collective-permute-done.1.below_ref.cls_below_ref = f32[27,8,256]{2,1,0:T(8,128)S(1)} collective-permute-done((f32[27,8,256]{2,1,0:T(8,128)}, f32[27,8,256]{2,1,0:T(8,128)S(1)}, u32[]{:S(2)}, u32[]{:S(2)}) %collective-permute-start.1) | collective-permute-done | bytes 221216 | tf_op jit(solution)/shard_map/ppermute | solution.py:446
  42.8 0.0 copy-start.1
  42.8 0.0 copy-done
  42.8 0.7 copy-done.1
  43.5 26.8 %phase0.1 = (f32[2,32,128]{2,1,0:T(8,128)}, f32[32,8,256]{2,1,0:T(8,128)}, f32[27,8,256]{2,1,0:T(8,128)}, f32[27,8,256]{2,1,0:T(8,128)}) custom-call(s32[3]{0:T(128)} %pad_add_fusion.scalars_ref, f32[27,8,256]{2,1,0:T(8,128)} %copy-done, f32[32,8,256]{2,1,0:T(8,128)} %get-tuple-element.21.tile_ref, f32[27,8,256]{2,1,0:T(8,128)} %copy-done.1, ...), custom_call_target="tpu_custom_call" | custom-call | tf_op jit(solution)/shard_map/phase0/pallas_call | solution.py:469
  70.3 5.6 %collective-permute-start.2 = (f32[27,8,256]{2,1,0:T(8,128)}, f32[27,8,256]{2,1,0:T(8,128)S(1)}, u32[]{:S(2)}, u32[]{:S(2)}) collective-permute-start(f32[27,8,256]{2,1,0:T(8,128)} %get-tuple-element.25), channel_id=1, source_target_pairs={{0,2},{1,3},{2,4},{3,5},{4,6},{5,7},{6,8},{7,9},{8,10},{9,11},{10,... | collective-permute-start | bytes 663560 | tf_op jit(solution)/shard_map/ppermute | solution.py:445
  76.0 3.2 %collective-permute-start.3 = (f32[27,8,256]{2,1,0:T(8,128)}, f32[27,8,256]{2,1,0:T(8,128)S(1)}, u32[]{:S(2)}, u32[]{:S(2)}) collective-permute-start(f32[27,8,256]{2,1,0:T(8,128)} %get-tuple-element.27), channel_id=1, source_target_pairs={{2,0},{3,1},{4,2},{5,3},{6,4},{7,5},{8,6},{9,7},{10,8},{11,9},{12,... | collective-permute-start | bytes 663560 | tf_op jit(solution)/shard_map/ppermute | solution.py:446
  79.2 2.9 %collective-permute-done.2.above_ref = f32[27,8,256]{2,1,0:T(8,128)S(1)} collective-permute-done((f32[27,8,256]{2,1,0:T(8,128)}, f32[27,8,256]{2,1,0:T(8,128)S(1)}, u32[]{:S(2)}, u32[]{:S(2)}) %collective-permute-start.2) | collective-permute-done | bytes 221216 | tf_op jit(solution)/shard_map/ppermute | solution.py:445
  82.1 0.0 copy-start.3
  82.1 7.6 %collective-permute-done.3.below_ref = f32[27,8,256]{2,1,0:T(8,128)S(1)} collective-permute-done((f32[27,8,256]{2,1,0:T(8,128)}, f32[27,8,256]{2,1,0:T(8,128)S(1)}, u32[]{:S(2)}, u32[]{:S(2)}) %collective-permute-start.3) | collective-permute-done | bytes 221216 | tf_op jit(solution)/shard_map/ppermute | solution.py:446
  89.7 0.0 copy-start.4
  89.7 0.0 copy-done.3
  89.7 0.7 copy-done.4
  90.4 46.0 %phase1.1 = (f32[3,32,128]{2,1,0:T(8,128)}, f32[32,8,128]{2,1,0:T(8,128)}, f32[27,8,128]{2,1,0:T(8,128)}, f32[27,8,128]{2,1,0:T(8,128)}) custom-call(s32[3]{0:T(128)} %pad_add_fusion.scalars_ref, f32[27,8,256]{2,1,0:T(8,128)} %copy-done.3, f32[32,8,256]{2,1,0:T(8,128)} %get-tuple-element.26.tile_ref, f32[27,8,256]{2,1,0:T(8,128)} %copy-done.4, ...), custom_call_target="tpu_custom_call" | custom-call | tf_op jit(solution)/shard_map/phase1/pallas_call | solution.py:469
  136.4 5.5 %collective-permute-start.4 = (f32[27,8,128]{2,1,0:T(8,128)}, f32[27,8,128]{2,1,0:T(8,128)S(1)}, u32[]{:S(2)}, u32[]{:S(2)}) collective-permute-start(f32[27,8,128]{2,1,0:T(8,128)} %get-tuple-element.29), channel_id=1, source_target_pairs={{0,2},{1,3},{2,4},{3,5},{4,6},{5,7},{6,8},{7,9},{8,10},{9,11},{10,... | collective-permute-start | bytes 331784 | tf_op jit(solution)/shard_map/ppermute | solution.py:445
  141.9 3.3 %collective-permute-start.5 = (f32[27,8,128]{2,1,0:T(8,128)}, f32[27,8,128]{2,1,0:T(8,128)S(1)}, u32[]{:S(2)}, u32[]{:S(2)}) collective-permute-start(f32[27,8,128]{2,1,0:T(8,128)} %get-tuple-element.31), channel_id=1, source_target_pairs={{2,0},{3,1},{4,2},{5,3},{6,4},{7,5},{8,6},{9,7},{10,8},{11,9},{12,... | collective-permute-start | bytes 331784 | tf_op jit(solution)/shard_map/ppermute | solution.py:446
  145.2 1.9 narrow.1
  147.2 0.0 collective-permute-done.4.above_ref
  147.2 0.0 copy-start.5
  147.2 2.6 %collective-permute-done.5.below_ref = f32[27,8,128]{2,1,0:T(8,128)S(1)} collective-permute-done((f32[27,8,128]{2,1,0:T(8,128)}, f32[27,8,128]{2,1,0:T(8,128)S(1)}, u32[]{:S(2)}, u32[]{:S(2)}) %collective-permute-start.5) | collective-permute-done | bytes 110624 | tf_op jit(solution)/shard_map/ppermute | solution.py:446
  149.8 0.0 copy-start.6
  149.8 0.0 copy-done.5
  149.8 0.6 copy-done.6
  150.4 0.0 copy-start.7
  150.4 0.0 copy-start.8
  150.4 36.6 %phase2.1 = f32[3,32,128]{2,1,0:T(8,128)} custom-call(s32[3]{0:T(128)} %pad_add_fusion.scalars_ref, f32[27,8,128]{2,1,0:T(8,128)} %copy-done.5, f32[32,8,128]{2,1,0:T(8,128)} %get-tuple-element.30.tile_ref, f32[27,8,128]{2,1,0:T(8,128)} %copy-done.6, f32[9,8,128]{2,1,0:T(8,128)} %get-tuple-element.32.cls_above_ref, f32[32,8,128]{2,1,0:T(8,128)} %get-tuple-element.33.cls_ref, ...), custom_call_target="tpu_custom_call" | custom-call | tf_op jit(solution)/shard_map/phase2/pallas_call | solution.py:469
  187.0 0.0 copy-done.7
  187.0 0.0 copy-done.8
  187.0 0.8 pad_maximum_fusion
  187.8 9.8 %all_to_all.10.in_ref = f32[16,16,128]{2,1,0:T(8,128)} all-to-all(f32[16,16,128]{2,1,0:T(8,128)S(1)} %bitcast.9), channel_id=1, replica_groups={{0,1,64,65,128,129,192,193,256,257,320,321,384,385,448,449},{2,3,66,67,..., dimensions={0} | all-to-all | bytes 262144 | tf_op jit(solution)/shard_map/all_to_all | solution.py:481
  197.6 1.6 collect.1
  (1 shorter events, 0.0 us)
Async XLA Ops:
  1.9 5.9 %copy-start.9 = (f32[2,8,2,10]{3,2,1,0:T(2,128)S(1)}, f32[2,8,2,10]{3,2,1,0:T(2,128)}, u32[]{:S(2)}) copy-start(f32[2,8,2,10]{3,2,1,0:T(2,128)} %param.6) | copy-start | bytes 3844
  1.9 15.8 %all-to-all-start = ((f32[16,32,256]{2,1,0:T(8,128)}), f32[16,32,256]{2,1,0:T(8,128)S(1)}, u32[]{:S(2)}, u32[]{:S(2)}) async-start(f32[16,32,256]{2,1,0:T(8,128)} %scatter.1), calls=%async_computation | async-start | bytes 1048576 | tf_op jit(solution)/shard_map/all_to_all | solution.py:424
  17.7 0.8 copy-start.2
  20.7 17.2 %collective-permute-start = (f32[27,8,256]{2,1,0:T(8,128)}, f32[27,8,256]{2,1,0:T(8,128)S(1)}, u32[]{:S(2)}, u32[]{:S(2)}) collective-permute-start(f32[27,8,256]{2,1,0:T(8,128)} %get-tuple-element.20), channel_id=1, source_target_pairs={{0,2},{1,3},{2,4},{3,5},{4,6},{5,7},{6,8},{7,9},{8,10},{9,11},{10,... | collective-permute-start | bytes 663560 | tf_op jit(solution)/shard_map/ppermute | solution.py:445
  25.9 16.9 %collective-permute-start.1 = (f32[27,8,256]{2,1,0:T(8,128)}, f32[27,8,256]{2,1,0:T(8,128)S(1)}, u32[]{:S(2)}, u32[]{:S(2)}) collective-permute-start(f32[27,8,256]{2,1,0:T(8,128)} %get-tuple-element.22), channel_id=1, source_target_pairs={{2,0},{3,1},{4,2},{5,3},{6,4},{7,5},{8,6},{9,7},{10,8},{11,9},{12,... | collective-permute-start | bytes 663560 | tf_op jit(solution)/shard_map/ppermute | solution.py:446
  33.8 0.7 copy-start.10
  38.0 4.9 %copy-start = (f32[27,8,256]{2,1,0:T(8,128)}, f32[27,8,256]{2,1,0:T(8,128)S(1)}, u32[]{:S(2)}) copy-start(f32[27,8,256]{2,1,0:T(8,128)S(1)} %collective-permute-done.above_ref.cls_above_ref) | copy-start | bytes 663556
  42.8 0.7 copy-start.1
  70.3 11.8 %collective-permute-start.2 = (f32[27,8,256]{2,1,0:T(8,128)}, f32[27,8,256]{2,1,0:T(8,128)S(1)}, u32[]{:S(2)}, u32[]{:S(2)}) collective-permute-start(f32[27,8,256]{2,1,0:T(8,128)} %get-tuple-element.25), channel_id=1, source_target_pairs={{0,2},{1,3},{2,4},{3,5},{4,6},{5,7},{6,8},{7,9},{8,10},{9,11},{10,... | collective-permute-start | bytes 663560 | tf_op jit(solution)/shard_map/ppermute | solution.py:445
  76.0 13.7 %collective-permute-start.3 = (f32[27,8,256]{2,1,0:T(8,128)}, f32[27,8,256]{2,1,0:T(8,128)S(1)}, u32[]{:S(2)}, u32[]{:S(2)}) collective-permute-start(f32[27,8,256]{2,1,0:T(8,128)} %get-tuple-element.27), channel_id=1, source_target_pairs={{2,0},{3,1},{4,2},{5,3},{6,4},{7,5},{8,6},{9,7},{10,8},{11,9},{12,... | collective-permute-start | bytes 663560 | tf_op jit(solution)/shard_map/ppermute | solution.py:446
  82.1 7.6 %copy-start.3 = (f32[27,8,256]{2,1,0:T(8,128)}, f32[27,8,256]{2,1,0:T(8,128)S(1)}, u32[]{:S(2)}) copy-start(f32[27,8,256]{2,1,0:T(8,128)S(1)} %collective-permute-done.2.above_ref) | copy-start | bytes 663556
  89.7 0.7 copy-start.4
  136.4 10.8 %collective-permute-start.4 = (f32[27,8,128]{2,1,0:T(8,128)}, f32[27,8,128]{2,1,0:T(8,128)S(1)}, u32[]{:S(2)}, u32[]{:S(2)}) collective-permute-start(f32[27,8,128]{2,1,0:T(8,128)} %get-tuple-element.29), channel_id=1, source_target_pairs={{0,2},{1,3},{2,4},{3,5},{4,6},{5,7},{6,8},{7,9},{8,10},{9,11},{10,... | collective-permute-start | bytes 331784 | tf_op jit(solution)/shard_map/ppermute | solution.py:445
  141.9 7.9 %collective-permute-start.5 = (f32[27,8,128]{2,1,0:T(8,128)}, f32[27,8,128]{2,1,0:T(8,128)S(1)}, u32[]{:S(2)}, u32[]{:S(2)}) collective-permute-start(f32[27,8,128]{2,1,0:T(8,128)} %get-tuple-element.31), channel_id=1, source_target_pairs={{2,0},{3,1},{4,2},{5,3},{6,4},{7,5},{8,6},{9,7},{10,8},{11,9},{12,... | collective-permute-start | bytes 331784 | tf_op jit(solution)/shard_map/ppermute | solution.py:446
  147.2 2.6 %copy-start.5 = (f32[27,8,128]{2,1,0:T(8,128)}, f32[27,8,128]{2,1,0:T(8,128)S(1)}, u32[]{:S(2)}) copy-start(f32[27,8,128]{2,1,0:T(8,128)S(1)} %collective-permute-done.4.above_ref) | copy-start | bytes 331780
  149.8 0.6 copy-start.6
  150.4 36.6 %copy-start.7 = (f32[3,32,128]{2,1,0:T(8,128)S(1)}, f32[3,32,128]{2,1,0:T(8,128)}, u32[]{:S(2)}) copy-start(f32[3,32,128]{2,1,0:T(8,128)} %get-tuple-element.28) | copy-start | bytes 147460
  150.4 36.6 %copy-start.8 = (f32[2,32,128]{2,1,0:T(8,128)S(1)}, f32[2,32,128]{2,1,0:T(8,128)}, u32[]{:S(2)}) copy-start(f32[2,32,128]{2,1,0:T(8,128)} %get-tuple-element.24) | copy-start | bytes 98308

commit v2 on v1

--- a/solution.py
+++ b/solution.py
@@ -11,35 +11,26 @@
 CLASSES = 8
 FIELDS = 8
 LANES = 128
-FUSED = 3
-LAG = 2
-UNROLL = 8
+BLOCK = 32
 PHASES = (2, 3, 3)
 TILE_ROWS = 32
 TILE_COLS = 64
 WIDE = 256
 ORIGIN = (WIDE - TILE_COLS) // 2
-PAD = 2
+PAD = 8
 
 
 def lane_ids():
     return lax.broadcasted_iota(jnp.int32, (FIELDS, LANES), 1)
 
 
-def inside(first_col, col_limit):
-    cols = lane_ids() + first_col
-    return jnp.where((cols >= 0) & (cols < col_limit), 0.25, 0.0).astype(jnp.float32)
-
-
-def blurred(parts, lane):
-    ahead = [pltpu.roll(x, LANES - 1, 1) for x in parts]
-    if len(parts) == 2:
-        ahead = [jnp.where(lane == LANES - 1, ahead[1], ahead[0]), ahead[1]]
-    pair = [x + y for x, y in zip(parts, ahead)]
-    behind = [pltpu.roll(x, 1, 1) for x in pair]
-    if len(parts) == 2:
-        behind = [behind[0], jnp.where(lane == 0, behind[0], behind[1])]
-    return [x + y for x, y in zip(pair, behind)]
+def column_matrix(first_col, col_limit, width):
+    source = lax.broadcasted_iota(jnp.int32, (width, width), 0)
+    target = lax.broadcasted_iota(jnp.int32, (width, width), 1)
+    apart = jnp.abs(source - target)
+    weight = jnp.where(apart == 0, 0.5, jnp.where(apart == 1, 0.25, 0.0))
+    cols = target + first_col
+    return jnp.where((cols >= 0) & (cols < col_limit), weight, 0.0).astype(jnp.bfloat16)
 
 
 def swapped(x, sub):
@@ -48,107 +39,76 @@
     return jnp.where(sub % 2 == 0, up, down)
 
 
-def sweep(first_degree, low, high, tiles, refs, tabs, scale):
-    cur, summed, acc, crs, idx = refs
-    lane = lane_ids()
+def pieces(x):
+    high = x.astype(jnp.bfloat16)
+    rest = x - high.astype(jnp.float32)
+    middle = rest.astype(jnp.bfloat16)
+    low = (rest - middle.astype(jnp.float32)).astype(jnp.bfloat16)
+    return jnp.concatenate([high, middle, low], axis=0)
+
+
+def one_pass(degree, low, high, terms, matrix_ref):
+    count = high - low
+    blocks = -(-count // BLOCK)
+    size = 2 * -(-count // (2 * blocks))
+    width = terms.shape[-1]
+
+    def block(i, _):
+        base = low + i * size
+        x = terms[degree, pl.ds(base - 1, size + 2)]
+        pair = x[:-1] + x[1:]
+        both = (pair[:-1] + pair[1:]).reshape((size * FIELDS, width))
+        parts = jnp.dot(pieces(both), matrix_ref[...], preferred_element_type=jnp.float32)
+        rows = size * FIELDS
+        blurred = (parts[:rows] + parts[rows : 2 * rows]) + parts[2 * rows :]
+        blurred = blurred.reshape((size, FIELDS, width))
+        here = x[1:-1]
+        if degree == 0:
+            following = 0.5 * blurred - here
+        else:
+            following = (blurred - (here + here)) - terms[degree - 1, pl.ds(base, size)]
+        terms[degree + 1, pl.ds(base, size)] = following
+        return 0
+
+    lax.fori_loop(0, blocks, block, 0)
+
+
+def weigh(low, high, tiles, terms, coef, idx, tab_ref):
     sub = lax.broadcasted_iota(jnp.int32, (FIELDS, LANES), 0)
-    opening = first_degree == 0
-    closing = first_degree + FUSED == PASSES
-    span = range(tiles)
-
-    def row(ref, at):
-        return [ref[at, :, t * LANES : (t + 1) * LANES] for t in span]
-
-    def put(ref, at, parts):
-        for t in span:
-            ref[at, :, t * LANES : (t + 1) * LANES] = parts[t]
-
-    def step(base, offset, live, valid=None):
-        at = base + offset
-        live[("t", 0, offset + 1)] = row(cur, at + 1)
-        for level in range(FUSED, 0, -1) if LAG > 1 else range(1, FUSED + 1):
-            own = offset - (level - 1) * LAG
-            if valid is not None and own < valid + level:
-                if level == 1 or own >= valid + level - 1:
-                    pass
-                continue
-            here = live[("t", level - 1, own)]
-            after = live[("t", level - 1, own + 1)]
-            pair = [x + y for x, y in zip(here, after)]
-            both = [x + y for x, y in zip(live[("u", level - 1, own - 1)], pair)]
-            live[("u", level - 1, own)] = pair
-            both = blurred(both, lane)
-            if opening and level == 1:
-                total = [(0.5 * s) * x for s, x in zip(scale, both)]
-            else:
-                before = row(summed, at) if level == 1 else live[("e", level - 1, own)]
-                total = [s * x - e for s, x, e in zip(scale, both, before)]
-            live[("e", level, own)] = total
-            live[("t", level, own)] = [e - x for e, x in zip(total, here)]
-        done = offset - (FUSED - 1) * LAG
-        if valid is not None and done < valid + FUSED:
-            return
-        place = base + done
-        picks = row(idx, place)
-        levels = list(range(0 if opening else 1, FUSED + 1))
-        terms = [row(cur, place) if level == 0 else live[("t", level, done)] for level in levels]
-        new_acc = [None] * tiles if opening else row(acc, place)
-        new_crs = [None] * tiles if opening else row(crs, place)
-        for level, term in zip(levels, terms):
-            real_tab, imag_tab = tabs(first_degree + level)
-            for t in span:
-                real = jnp.take_along_axis(real_tab, picks[t], axis=1) * term[t]
-                imag = jnp.take_along_axis(imag_tab, picks[t], axis=1) * term[t]
-                new_acc[t] = real if new_acc[t] is None else new_acc[t] + real
-                new_crs[t] = imag if new_crs[t] is None else new_crs[t] + imag
-        if closing:
-            put(cur, place, [x + swapped(y, sub) for x, y in zip(new_acc, new_crs)])
-        else:
-            put(acc, place, new_acc)
-            put(crs, place, new_crs)
-            put(cur, place, live[("t", FUSED, done)])
-            put(summed, place, live[("e", FUSED, done)])
-
-    def seed(live, valid, offset):
-        for level in range(1, FUSED):
-            edge = valid + level
-            one, two = ("t", level, edge), ("t", level, edge + 1)
-            if one in live and two in live and ("u", level, edge) not in live:
-                live[("u", level, edge)] = [x + y for x, y in zip(live[one], live[two])]
-
-    def keys(offset):
-        out = [("t", 0, offset), ("u", 0, offset - 1)]
-        for level in range(1, FUSED):
-            newest = offset - 1 - (level - 1) * LAG
-            for r in range(offset - (FUSED - 1) * LAG, newest + 1):
-                out.append(("t", level, r))
-            for r in range(offset - level * LAG, newest + 1):
-                out.append(("e", level, r))
-            out.append(("u", level, offset - level * LAG - 1))
-        return out
-
-    start = FUSED + (FUSED - 1) * LAG
-    live = {("t", 0, 0): row(cur, low), ("t", 0, 1): row(cur, low + 1)}
-    live[("u", 0, 0)] = [x + y for x, y in zip(live[("t", 0, 0)], live[("t", 0, 1)])]
-    for offset in range(1, start):
-        step(low, offset, live, valid=0)
-        seed(live, 0, offset)
-    count = high - low - 2 * FUSED
-    carry = [live[key] for key in keys(start)]
-
-    def block(base, carry, length):
-        live = dict(zip(keys(0), carry))
-        for offset in range(length):
-            step(base, offset, live)
-        return [live[key] for key in keys(length)]
-
-    def body(i, carry):
-        return block(low + start + i * UNROLL, carry, UNROLL)
-
-    whole = count // UNROLL
-    carry = lax.fori_loop(0, whole, body, carry)
-    if count % UNROLL:
-        block(low + start + whole * UNROLL, carry, count % UNROLL)
+    signs = jnp.where((sub % 4 == 0) | (sub % 4 == 3), 1.0, -1.0)
+
+    def pick(i, _):
+        for t in range(tiles):
+            here = slice(t * LANES, (t + 1) * LANES)
+            picks = idx[low + i, :, here]
+            for g in range(tab_ref.shape[0]):
+                found = jnp.take_along_axis(tab_ref[g], picks, axis=1, mode="promise_in_bounds")
+                coef[low + i, g * FIELDS : (g + 1) * FIELDS, here] = found
+        return 0
+
+    lax.fori_loop(0, high - low, pick, 0, unroll=2)
+
+    def combine(i, _):
+        at = low + i
+        for t in range(tiles):
+            here = slice(t * LANES, (t + 1) * LANES)
+
+            def one(degree, part):
+                first = 4 * degree + 2 * part
+                a = jnp.broadcast_to(coef[at, first : first + 1, here], (FIELDS, LANES))
+                b = jnp.broadcast_to(coef[at, first + 1 : first + 2, here], (FIELDS, LANES))
+                return jnp.where(sub < FIELDS // 2, a, b)
+
+            own, other = None, None
+            for degree in range(PASSES + 1):
+                term = terms[degree, at, :, here]
+                real, imag = one(degree, 0) * term, one(degree, 1) * term
+                own = real if own is None else own + real
+                other = imag if other is None else other + imag
+            terms[0, at, :, here] = own + swapped(signs * other, sub)
+        return 0
+
+    lax.fori_loop(0, high - low, combine, 0, unroll=2)
 
 
 def centred(parts, lane):
@@ -158,11 +118,12 @@
     return jnp.where(lane < LANES // 2, left, right)
 
 
-def run_phase(steps, first_depth, tiles, flags, cur, refs, classes, tab_ref, image_ref, scale):
+def run_phase(steps, first_depth, tiles, flags, terms, refs, classes, tab_ref, image_ref):
     halo = steps * PASSES
     lane = lane_ids()
     sub = lax.broadcasted_iota(jnp.int32, (FIELDS, LANES), 0)
-    summed, acc, crs, idx = refs
+    matrix_ref, coef, idx = refs
+    cur = terms.at[0]
     total = TILE_ROWS + 2 * halo
 
     @pl.when(flags[0] == 1)
@@ -177,9 +138,6 @@
         cur[end] = jnp.zeros_like(cur[0])
         for i in range(1, halo):
             cur[end + i] = -cur[end - i]
-
-    def tabs(degree):
-        return tab_ref[degree, 0], tab_ref[degree, 1]
 
     for local in range(steps):
         reach = (steps - 1 - local) * PASSES
@@ -208,16 +166,9 @@
                     idx[end + i] = idx[end - i]
 
         low, high = local * PASSES, total - local * PASSES
-        for part in range(PASSES // FUSED):
-            sweep(
-                part * FUSED,
-                low + part * FUSED,
-                high - part * FUSED,
-                tiles,
-                (cur, summed, acc, crs, idx),
-                tabs,
-                scale,
-            )
+        for degree in range(PASSES):
+            one_pass(degree, low + degree + 1, high - degree - 1, terms, matrix_ref)
+        weigh(low + PASSES, high - PASSES, tiles, terms, coef, idx, tab_ref)
 
         def pictured(i, _):
             parts = [cur[halo + i, :, t * LANES : (t + 1) * LANES] for t in range(tiles)]
@@ -311,21 +262,22 @@
     tiles = tile_ref.shape[-1] // LANES
     last = phase == len(PHASES) - 1
     if last:
-        image_ref, cur, *refs = rest
+        image_ref, terms, *refs = rest
     else:
-        image_ref, out_ref, up_ref, down_ref, cur, *refs = rest
+        image_ref, out_ref, up_ref, down_ref, terms, *refs = rest
+    cur = terms.at[0]
     cur[0:halo] = above_ref[0:halo]
     cur[halo : halo + TILE_ROWS] = tile_ref[...]
     cur[halo + TILE_ROWS : TILE_ROWS + 2 * halo] = below_ref[0:halo]
     first_col = scalars_ref[2] - (ORIGIN if tiles == 2 else ORIGIN - LANES // 2)
-    scale = [inside(first_col + t * LANES, col_limit) for t in range(tiles)]
+    refs[0][...] = column_matrix(first_col, col_limit, tiles * LANES)
     reader = class_rows(
         cls_above_ref, cls_ref, cls_below_ref, PHASES[0] * PASSES if not classes_narrow else 0,
         slice(0, tiles * LANES),
     )
     run_phase(
-        steps, sum(PHASES[:phase]), tiles, (scalars_ref[0], scalars_ref[1]), cur, refs, reader,
-        tab_ref, image_ref, scale,
+        steps, sum(PHASES[:phase]), tiles, (scalars_ref[0], scalars_ref[1]), terms, refs, reader,
+        tab_ref, image_ref,
     )
     if last:
         return
@@ -367,11 +319,8 @@
 
 
 def coefficient_tables(table):
-    by_field = jnp.repeat(jnp.transpose(table, (3, 2, 0, 1)), 4, axis=2)
-    signs = jnp.array([1.0, -1.0, -1.0, 1.0] * 2, jnp.float32)
-    parts = jnp.stack([jnp.ones_like(signs), signs])
-    by_field = by_field * parts[None, :, :, None]
-    return jnp.pad(by_field, ((0, 0), (0, 0), (0, 0), (0, LANES - CLASSES)))
+    rows = jnp.transpose(table, (3, 2, 0, 1)).reshape((-1, FIELDS, CLASSES))
+    return jnp.pad(rows, ((0, 0), (0, 0), (0, LANES - CLASSES)))
 
 
 VMEM = pl.BlockSpec(memory_space=pltpu.VMEM)
@@ -387,6 +336,17 @@
     return pl.pallas_call(
         kernel, out_shape=out_shape, in_specs=in_specs, out_specs=outs, scratch_shapes=scratch, name=name
     )
+
+
+def phase_scratch(phase):
+    rows = TILE_ROWS + 2 * PHASES[phase] * PASSES + PAD
+    width = LANES if phase == len(PHASES) - 1 else WIDE
+    return [
+        pltpu.VMEM((PASSES + 1, rows, FIELDS, width), jnp.float32),
+        pltpu.VMEM((width, width), jnp.bfloat16),
+        pltpu.VMEM((rows, 4 * (PASSES + 1), width), jnp.float32),
+        pltpu.VMEM((rows, FIELDS, width), jnp.int32),
+    ]
 
 
 def body(surface, velocity_class, table):
@@ -445,7 +405,6 @@
         above = lax.ppermute(down, "strip", ahead)
         below = lax.ppermute(up, "strip", back)
         last = phase == len(PHASES) - 1
-        width = LANES if last else WIDE
         if phase == 0:
             class_args = (above, classes, below)
             narrow_args = call(
@@ -458,14 +417,12 @@
                 [VMEM] * 3,
                 name="narrow",
             )(*class_args)
-        rows = TILE_ROWS + 2 * halos[phase]
         out_shape = [shaped(steps, TILE_ROWS, LANES)]
         if not last:
             next_width = LANES if phase + 1 == len(PHASES) - 1 else WIDE
             out_shape.append(shaped(TILE_ROWS, FIELDS, next_width))
             out_shape += [shaped(halos[phase + 1], FIELDS, next_width)] * 2
-        scratch = [pltpu.VMEM((rows + PAD, FIELDS, width), jnp.float32)] * 4
-        scratch.append(pltpu.VMEM((rows + PAD, FIELDS, width), jnp.int32))
+        scratch = phase_scratch(phase)
         out = call(
             functools.partial(phase_kernel, phase, columns, last),
             tuple(out_shape),

time: 201 us -> 165 us (0.82)
  Pallas kernels: 117 us -> 82 us
  blocking collectives: 9.81 us -> 25.5 us
  waiting for transfers between devices: 29.8 us -> 20.8 us
  starting transfers between devices: 36.6 us -> 30.7 us
    pallas_call x3, Pallas kernels: 109 us -> 74.3 us  [body(): call(functools.partial(phase_kernel, phase, columns, last), tuple(out_sha...]
    all_to_all x0 -> x1, blocking collectives: none -> 15.7 us  [body(): lax.all_to_all(outgoing, both_axes, 0, 0, axis_index_groups=groups, tiled...]
    all_to_all x1 -> x0, waiting for transfers between devices: 9.75 us -> none  [body(): lax.all_to_all(outgoing, both_axes, 0, 0, axis_index_groups=groups, tiled...]
    all_to_all x1 -> x0, starting transfers between devices: 5.89 us -> none  [body(): lax.all_to_all(outgoing, both_axes, 0, 0, axis_index_groups=groups, tiled...]
  transfers between devices with their start and end apart: 7 -> 6, of which waited for: 6 -> 5; matrix products, arithmetic and copies ran while one was open for 1% -> 1% of each run, Pallas kernels for 1% -> 1%
where the time goes in v2:
time: 165 us; the launch traced here: 163 us
  Pallas kernels  82 us (50%)
  starting transfers between devices  30.7 us (19%)
  blocking collectives  25.5 us (15%)
  waiting for transfers between devices  20.8 us (13%)
  local copies, waits for them, and re-layouts  2.73 us (2%)
    pallas_call x3, Pallas kernels, body(): call(functools.partial(phase_kernel, phase, columns, last), tuple(out_sha...  74.3 us
    ppermute x3, starting transfers between devices, body(): above = lax.ppermute(down, 'strip', ahead)  16.3 us
    all_to_all x1, blocking collectives, body(): lax.all_to_all(outgoing, both_axes, 0, 0, axis_index_groups=groups, tiled...  15.7 us
    ppermute x3, waiting for transfers between devices, body(): below = lax.ppermute(up, 'strip', back)  15 us
    ppermute x3, starting transfers between devices, body(): below = lax.ppermute(up, 'strip', back)  14.4 us
    all_to_all x1, blocking collectives, body(): lax.all_to_all(image, both_axes, 0, 0, axis_index_groups=groups, tiled=True)  9.8 us
    ppermute x3, waiting for transfers between devices, body(): above = lax.ppermute(down, 'strip', ahead)  5.78 us
  transfers between devices with their start and end apart: 6, of which 5 were waited for; matrix products, arithmetic and copies ran while one was open for 1% of the time, Pallas kernels for 1%

profile of v2, /device:TPU:24, one launch (start us, length us, event | category | flops | bytes accessed | tf_op | source)
XLA Modules:
  0.0 163.3 jit_solution(5439124477875351831)
XLA Ops:
  0.0 1.9 %scatter.1 = f32[16,32,256]{2,1,0:T(8,128)} custom-call(s32[1]{0:T(128)} %bitcast.3.part_ref, f32[8,16,1024]{2,1,0:T(8,128)} %bitcast.8, s32[1,16,1024]{2,1,0:T(8,128)} %velocity_ref.1), custom_call_target="tpu_custom_call" | custom-call | tf_op jit(solution)/shard_map/scatter/pallas_call | solution.py:369
  1.9 15.7 %all_to_all.10.in_ref = f32[16,32,256]{2,1,0:T(8,128)} all-to-all(f32[16,32,256]{2,1,0:T(8,128)} %scatter.1), channel_id=1, replica_groups={{0,1,64,65,128,129,192,193,256,257,320,321,384,385,448,449},{2,3,66,67,..., dimensions={0} | all-to-all | bytes 1048576 | tf_op jit(solution)/shard_map/all_to_all | solution.py:384
  17.7 2.2 %gather.1 = (f32[32,8,256]{2,1,0:T(8,128)}, f32[32,8,256]{2,1,0:T(8,128)}, f32[27,8,256]{2,1,0:T(8,128)}, f32[27,8,256]{2,1,0:T(8,128)}) custom-call(f32[16,32,256]{2,1,0:T(8,128)} %all_to_all.10.in_ref), custom_call_target="tpu_custom_call" | custom-call | tf_op jit(solution)/shard_map/gather/pallas_call | solution.py:388
  19.8 5.2 %collective-permute-start = (f32[27,8,256]{2,1,0:T(8,128)}, f32[27,8,256]{2,1,0:T(8,128)S(1)}, u32[]{:S(2)}, u32[]{:S(2)}) collective-permute-start(f32[27,8,256]{2,1,0:T(8,128)} %get-tuple-element.20), channel_id=1, source_target_pairs={{0,2},{1,3},{2,4},{3,5},{4,6},{5,7},{6,8},{7,9},{8,10},{9,11},{10,... | collective-permute-start | bytes 663560 | tf_op jit(solution)/shard_map/ppermute | solution.py:405
  25.0 0.0 copy-start.8
  25.0 7.9 %collective-permute-start.1 = (f32[27,8,256]{2,1,0:T(8,128)}, f32[27,8,256]{2,1,0:T(8,128)S(1)}, u32[]{:S(2)}, u32[]{:S(2)}) collective-permute-start(f32[27,8,256]{2,1,0:T(8,128)} %get-tuple-element.22), channel_id=1, source_target_pairs={{2,0},{3,1},{4,2},{5,3},{6,4},{7,5},{8,6},{9,7},{10,8},{11,9},{12,... | collective-permute-start | bytes 663560 | tf_op jit(solution)/shard_map/ppermute | solution.py:406
  32.9 0.0 copy-done.8
  32.9 0.1 copy.4
  33.0 0.6 pad.4.tab_ref
  33.7 0.6 pad_add_fusion.scalars_ref
  34.2 2.8 %collective-permute-done.above_ref.cls_above_ref = f32[27,8,256]{2,1,0:T(8,128)S(1)} collective-permute-done((f32[27,8,256]{2,1,0:T(8,128)}, f32[27,8,256]{2,1,0:T(8,128)S(1)}, u32[]{:S(2)}, u32[]{:S(2)}) %collective-permute-start) | collective-permute-done | bytes 221216 | tf_op jit(solution)/shard_map/ppermute | solution.py:405
  37.1 0.0 copy-start
  37.1 4.9 %collective-permute-done.1.below_ref.cls_below_ref = f32[27,8,256]{2,1,0:T(8,128)S(1)} collective-permute-done((f32[27,8,256]{2,1,0:T(8,128)}, f32[27,8,256]{2,1,0:T(8,128)S(1)}, u32[]{:S(2)}, u32[]{:S(2)}) %collective-permute-start.1) | collective-permute-done | bytes 221216 | tf_op jit(solution)/shard_map/ppermute | solution.py:406
  41.9 0.0 copy-start.1
  41.9 0.0 copy-done
  41.9 0.7 copy-done.1
  42.6 18.9 %phase0.1 = (f32[2,32,128]{2,1,0:T(8,128)}, f32[32,8,256]{2,1,0:T(8,128)}, f32[27,8,256]{2,1,0:T(8,128)}, f32[27,8,256]{2,1,0:T(8,128)}) custom-call(s32[3]{0:T(128)} %pad_add_fusion.scalars_ref, f32[27,8,256]{2,1,0:T(8,128)} %copy-done, f32[32,8,256]{2,1,0:T(8,128)} %get-tuple-element.21.tile_ref, f32[27,8,256]{2,1,0:T(8,128)} %copy-done.1, ...), custom_call_target="tpu_custom_call" | custom-call | tf_op jit(solution)/shard_map/phase0/pallas_call | solution.py:426
  61.5 5.6 %collective-permute-start.2 = (f32[27,8,256]{2,1,0:T(8,128)}, f32[27,8,256]{2,1,0:T(8,128)S(1)}, u32[]{:S(2)}, u32[]{:S(2)}) collective-permute-start(f32[27,8,256]{2,1,0:T(8,128)} %get-tuple-element.25), channel_id=1, source_target_pairs={{0,2},{1,3},{2,4},{3,5},{4,6},{5,7},{6,8},{7,9},{8,10},{9,11},{10,... | collective-permute-start | bytes 663560 | tf_op jit(solution)/shard_map/ppermute | solution.py:405
  67.1 3.2 %collective-permute-start.3 = (f32[27,8,256]{2,1,0:T(8,128)}, f32[27,8,256]{2,1,0:T(8,128)S(1)}, u32[]{:S(2)}, u32[]{:S(2)}) collective-permute-start(f32[27,8,256]{2,1,0:T(8,128)} %get-tuple-element.27), channel_id=1, source_target_pairs={{2,0},{3,1},{4,2},{5,3},{6,4},{7,5},{8,6},{9,7},{10,8},{11,9},{12,... | collective-permute-start | bytes 663560 | tf_op jit(solution)/shard_map/ppermute | solution.py:406
  70.4 2.9 %collective-permute-done.2.above_ref = f32[27,8,256]{2,1,0:T(8,128)S(1)} collective-permute-done((f32[27,8,256]{2,1,0:T(8,128)}, f32[27,8,256]{2,1,0:T(8,128)S(1)}, u32[]{:S(2)}, u32[]{:S(2)}) %collective-permute-start.2) | collective-permute-done | bytes 221216 | tf_op jit(solution)/shard_map/ppermute | solution.py:405
  73.3 0.0 copy-start.2
  73.3 7.6 %collective-permute-done.3.below_ref = f32[27,8,256]{2,1,0:T(8,128)S(1)} collective-permute-done((f32[27,8,256]{2,1,0:T(8,128)}, f32[27,8,256]{2,1,0:T(8,128)S(1)}, u32[]{:S(2)}, u32[]{:S(2)}) %collective-permute-start.3) | collective-permute-done | bytes 221216 | tf_op jit(solution)/shard_map/ppermute | solution.py:406
  80.9 0.0 copy-start.3
  80.9 0.0 copy-done.2
  80.9 0.7 copy-done.3
  81.5 31.9 %phase1.1 = (f32[3,32,128]{2,1,0:T(8,128)}, f32[32,8,128]{2,1,0:T(8,128)}, f32[27,8,128]{2,1,0:T(8,128)}, f32[27,8,128]{2,1,0:T(8,128)}) custom-call(s32[3]{0:T(128)} %pad_add_fusion.scalars_ref, f32[27,8,256]{2,1,0:T(8,128)} %copy-done.2, f32[32,8,256]{2,1,0:T(8,128)} %get-tuple-element.26.tile_ref, f32[27,8,256]{2,1,0:T(8,128)} %copy-done.3, ...), custom_call_target="tpu_custom_call" | custom-call | tf_op jit(solution)/shard_map/phase1/pallas_call | solution.py:426
  113.5 5.5 %collective-permute-start.4 = (f32[27,8,128]{2,1,0:T(8,128)}, f32[27,8,128]{2,1,0:T(8,128)S(1)}, u32[]{:S(2)}, u32[]{:S(2)}) collective-permute-start(f32[27,8,128]{2,1,0:T(8,128)} %get-tuple-element.29), channel_id=1, source_target_pairs={{0,2},{1,3},{2,4},{3,5},{4,6},{5,7},{6,8},{7,9},{8,10},{9,11},{10,... | collective-permute-start | bytes 331784 | tf_op jit(solution)/shard_map/ppermute | solution.py:405
  119.0 3.3 %collective-permute-start.5 = (f32[27,8,128]{2,1,0:T(8,128)}, f32[27,8,128]{2,1,0:T(8,128)S(1)}, u32[]{:S(2)}, u32[]{:S(2)}) collective-permute-start(f32[27,8,128]{2,1,0:T(8,128)} %get-tuple-element.31), channel_id=1, source_target_pairs={{2,0},{3,1},{4,2},{5,3},{6,4},{7,5},{8,6},{9,7},{10,8},{11,9},{12,... | collective-permute-start | bytes 331784 | tf_op jit(solution)/shard_map/ppermute | solution.py:406
  122.3 1.9 %narrow.1 = (f32[9,8,128]{2,1,0:T(8,128)}, f32[32,8,128]{2,1,0:T(8,128)}, f32[9,8,128]{2,1,0:T(8,128)}) custom-call(f32[27,8,256]{2,1,0:T(8,128)} %copy-done, f32[32,8,256]{2,1,0:T(8,128)} %get-tuple-element.23.cls_ref.own_ref, f32[27,8,256]{2,1,0:T(8,128)} %copy-done.1), custom_call_target="tpu_custom_call" | custom-call | tf_op jit(solution)/shard_map/narrow/pallas_call | solution.py:410
  124.3 0.0 collective-permute-done.4.above_ref
  124.3 0.0 copy-start.4
  124.3 2.6 %collective-permute-done.5.below_ref = f32[27,8,128]{2,1,0:T(8,128)S(1)} collective-permute-done((f32[27,8,128]{2,1,0:T(8,128)}, f32[27,8,128]{2,1,0:T(8,128)S(1)}, u32[]{:S(2)}, u32[]{:S(2)}) %collective-permute-start.5) | collective-permute-done | bytes 110624 | tf_op jit(solution)/shard_map/ppermute | solution.py:406
  126.9 0.0 copy-start.5
  126.9 0.0 copy-done.4
  126.9 0.6 copy-done.5
  127.5 0.0 copy-start.6
  127.5 0.0 copy-start.7
  127.5 23.5 %phase2.1 = f32[3,32,128]{2,1,0:T(8,128)} custom-call(s32[3]{0:T(128)} %pad_add_fusion.scalars_ref, f32[27,8,128]{2,1,0:T(8,128)} %copy-done.4, f32[32,8,128]{2,1,0:T(8,128)} %get-tuple-element.30.tile_ref, f32[27,8,128]{2,1,0:T(8,128)} %copy-done.5, f32[9,8,128]{2,1,0:T(8,128)} %get-tuple-element.32.cls_above_ref, f32[32,8,128]{2,1,0:T(8,128)} %get-tuple-element.33.cls_ref, ...), custom_call_target="tpu_custom_call" | custom-call | tf_op jit(solution)/shard_map/phase2/pallas_call | solution.py:426
  151.1 0.0 copy-done.6
  151.1 0.0 copy-done.7
  151.1 0.8 pad_maximum_fusion
  151.9 9.8 %all_to_all.11.in_ref = f32[16,16,128]{2,1,0:T(8,128)} all-to-all(f32[16,16,128]{2,1,0:T(8,128)S(1)} %bitcast.9), channel_id=1, replica_groups={{0,1,64,65,128,129,192,193,256,257,320,321,384,385,448,449},{2,3,66,67,..., dimensions={0} | all-to-all | bytes 262144 | tf_op jit(solution)/shard_map/all_to_all | solution.py:438
  161.7 1.6 %collect.1 = f32[1,16,1024]{2,1,0:T(8,128)} custom-call(f32[16,16,128]{2,1,0:T(8,128)} %all_to_all.11.in_ref), custom_call_target="tpu_custom_call" | custom-call | tf_op jit(solution)/shard_map/collect/pallas_call | solution.py:439
Async XLA Ops:
  19.8 17.2 %collective-permute-start = (f32[27,8,256]{2,1,0:T(8,128)}, f32[27,8,256]{2,1,0:T(8,128)S(1)}, u32[]{:S(2)}, u32[]{:S(2)}) collective-permute-start(f32[27,8,256]{2,1,0:T(8,128)} %get-tuple-element.20), channel_id=1, source_target_pairs={{0,2},{1,3},{2,4},{3,5},{4,6},{5,7},{6,8},{7,9},{8,10},{9,11},{10,... | collective-permute-start | bytes 663560 | tf_op jit(solution)/shard_map/ppermute | solution.py:405
  25.0 7.9 %copy-start.8 = (f32[2,8,2,10]{3,2,1,0:T(2,128)S(1)}, f32[2,8,2,10]{3,2,1,0:T(2,128)}, u32[]{:S(2)}) copy-start(f32[2,8,2,10]{3,2,1,0:T(2,128)} %param.5) | copy-start | bytes 3844
  25.0 16.9 %collective-permute-start.1 = (f32[27,8,256]{2,1,0:T(8,128)}, f32[27,8,256]{2,1,0:T(8,128)S(1)}, u32[]{:S(2)}, u32[]{:S(2)}) collective-permute-start(f32[27,8,256]{2,1,0:T(8,128)} %get-tuple-element.22), channel_id=1, source_target_pairs={{2,0},{3,1},{4,2},{5,3},{6,4},{7,5},{8,6},{9,7},{10,8},{11,9},{12,... | collective-permute-start | bytes 663560 | tf_op jit(solution)/shard_map/ppermute | solution.py:406
  37.1 4.9 %copy-start = (f32[27,8,256]{2,1,0:T(8,128)}, f32[27,8,256]{2,1,0:T(8,128)S(1)}, u32[]{:S(2)}) copy-start(f32[27,8,256]{2,1,0:T(8,128)S(1)} %collective-permute-done.above_ref.cls_above_ref) | copy-start | bytes 663556
  41.9 0.7 copy-start.1
  61.5 11.8 %collective-permute-start.2 = (f32[27,8,256]{2,1,0:T(8,128)}, f32[27,8,256]{2,1,0:T(8,128)S(1)}, u32[]{:S(2)}, u32[]{:S(2)}) collective-permute-start(f32[27,8,256]{2,1,0:T(8,128)} %get-tuple-element.25), channel_id=1, source_target_pairs={{0,2},{1,3},{2,4},{3,5},{4,6},{5,7},{6,8},{7,9},{8,10},{9,11},{10,... | collective-permute-start | bytes 663560 | tf_op jit(solution)/shard_map/ppermute | solution.py:405
  67.1 13.7 %collective-permute-start.3 = (f32[27,8,256]{2,1,0:T(8,128)}, f32[27,8,256]{2,1,0:T(8,128)S(1)}, u32[]{:S(2)}, u32[]{:S(2)}) collective-permute-start(f32[27,8,256]{2,1,0:T(8,128)} %get-tuple-element.27), channel_id=1, source_target_pairs={{2,0},{3,1},{4,2},{5,3},{6,4},{7,5},{8,6},{9,7},{10,8},{11,9},{12,... | collective-permute-start | bytes 663560 | tf_op jit(solution)/shard_map/ppermute | solution.py:406
  73.3 7.6 %copy-start.2 = (f32[27,8,256]{2,1,0:T(8,128)}, f32[27,8,256]{2,1,0:T(8,128)S(1)}, u32[]{:S(2)}) copy-start(f32[27,8,256]{2,1,0:T(8,128)S(1)} %collective-permute-done.2.above_ref) | copy-start | bytes 663556
  80.9 0.7 copy-start.3
  113.5 10.8 %collective-permute-start.4 = (f32[27,8,128]{2,1,0:T(8,128)}, f32[27,8,128]{2,1,0:T(8,128)S(1)}, u32[]{:S(2)}, u32[]{:S(2)}) collective-permute-start(f32[27,8,128]{2,1,0:T(8,128)} %get-tuple-element.29), channel_id=1, source_target_pairs={{0,2},{1,3},{2,4},{3,5},{4,6},{5,7},{6,8},{7,9},{8,10},{9,11},{10,... | collective-permute-start | bytes 331784 | tf_op jit(solution)/shard_map/ppermute | solution.py:405
  119.0 7.9 %collective-permute-start.5 = (f32[27,8,128]{2,1,0:T(8,128)}, f32[27,8,128]{2,1,0:T(8,128)S(1)}, u32[]{:S(2)}, u32[]{:S(2)}) collective-permute-start(f32[27,8,128]{2,1,0:T(8,128)} %get-tuple-element.31), channel_id=1, source_target_pairs={{2,0},{3,1},{4,2},{5,3},{6,4},{7,5},{8,6},{9,7},{10,8},{11,9},{12,... | collective-permute-start | bytes 331784 | tf_op jit(solution)/shard_map/ppermute | solution.py:406
  124.3 2.6 %copy-start.4 = (f32[27,8,128]{2,1,0:T(8,128)}, f32[27,8,128]{2,1,0:T(8,128)S(1)}, u32[]{:S(2)}) copy-start(f32[27,8,128]{2,1,0:T(8,128)S(1)} %collective-permute-done.4.above_ref) | copy-start | bytes 331780
  126.9 0.6 copy-start.5
  127.5 23.5 %copy-start.6 = (f32[3,32,128]{2,1,0:T(8,128)S(1)}, f32[3,32,128]{2,1,0:T(8,128)}, u32[]{:S(2)}) copy-start(f32[3,32,128]{2,1,0:T(8,128)} %get-tuple-element.28) | copy-start | bytes 147460
  127.5 23.5 %copy-start.7 = (f32[2,32,128]{2,1,0:T(8,128)S(1)}, f32[2,32,128]{2,1,0:T(8,128)}, u32[]{:S(2)}) copy-start(f32[2,32,128]{2,1,0:T(8,128)} %get-tuple-element.24) | copy-start | bytes 98308

commit v3 on v2

--- a/solution.py
+++ b/solution.py
@@ -50,8 +50,9 @@
 def one_pass(degree, low, high, terms, matrix_ref):
     count = high - low
     blocks = -(-count // BLOCK)
-    size = 2 * -(-count // (2 * blocks))
     width = terms.shape[-1]
+    step = 2 if width > LANES else 4
+    size = step * -(-count // (step * blocks))
 
     def block(i, _):
         base = low + i * size
@@ -86,7 +87,7 @@
                 coef[low + i, g * FIELDS : (g + 1) * FIELDS, here] = found
         return 0
 
-    lax.fori_loop(0, high - low, pick, 0, unroll=2)
+    lax.fori_loop(0, high - low, pick, 0, unroll=4)
 
     def combine(i, _):
         at = low + i
@@ -108,7 +109,7 @@
             terms[0, at, :, here] = own + swapped(signs * other, sub)
         return 0
 
-    lax.fori_loop(0, high - low, combine, 0, unroll=2)
+    lax.fori_loop(0, high - low, combine, 0, unroll=4)
 
 
 def centred(parts, lane):

time: 165 us -> 157 us (0.952)
  Pallas kernels: 82 us -> 73.8 us
    pallas_call x3, Pallas kernels: 74.3 us -> 66.1 us  [body(): call(functools.partial(phase_kernel, phase, columns, last), tuple(out_sha...]
where the time goes in v3:
time: 157 us; the launch traced here: 155 us
  Pallas kernels  73.8 us (47%)
  starting transfers between devices  30.7 us (20%)
  blocking collectives  25.5 us (16%)
  waiting for transfers between devices  20.8 us (13%)
  local copies, waits for them, and re-layouts  2.73 us (2%)
    pallas_call x3, Pallas kernels, body(): call(functools.partial(phase_kernel, phase, columns, last), tuple(out_sha...  66.1 us
    ppermute x3, starting transfers between devices, body(): above = lax.ppermute(down, 'strip', ahead)  16.3 us
    all_to_all x1, blocking collectives, body(): lax.all_to_all(outgoing, both_axes, 0, 0, axis_index_groups=groups, tiled...  15.7 us
    ppermute x3, waiting for transfers between devices, body(): below = lax.ppermute(up, 'strip', back)  15 us
    ppermute x3, starting transfers between devices, body(): below = lax.ppermute(up, 'strip', back)  14.4 us
    all_to_all x1, blocking collectives, body(): lax.all_to_all(image, both_axes, 0, 0, axis_index_groups=groups, tiled=True)  9.8 us
    ppermute x3, waiting for transfers between devices, body(): above = lax.ppermute(down, 'strip', ahead)  5.78 us
  transfers between devices with their start and end apart: 6, of which 5 were waited for; matrix products, arithmetic and copies ran while one was open for 1% of the time, Pallas kernels for 1%

profile of v3, /device:TPU:24, one launch (start us, length us, event | category | flops | bytes accessed | tf_op | source)
XLA Modules:
  0.0 155.1 jit_solution(8911313899701817305)
XLA Ops:
  0.0 1.9 %scatter.1 = f32[16,32,256]{2,1,0:T(8,128)} custom-call(s32[1]{0:T(128)} %bitcast.3.part_ref, f32[8,16,1024]{2,1,0:T(8,128)} %bitcast.8, s32[1,16,1024]{2,1,0:T(8,128)} %velocity_ref.1), custom_call_target="tpu_custom_call" | custom-call | tf_op jit(solution)/shard_map/scatter/pallas_call | solution.py:370
  1.9 15.7 %all_to_all.10.in_ref = f32[16,32,256]{2,1,0:T(8,128)} all-to-all(f32[16,32,256]{2,1,0:T(8,128)} %scatter.1), channel_id=1, replica_groups={{0,1,64,65,128,129,192,193,256,257,320,321,384,385,448,449},{2,3,66,67,..., dimensions={0} | all-to-all | bytes 1048576 | tf_op jit(solution)/shard_map/all_to_all | solution.py:385
  17.7 2.2 %gather.1 = (f32[32,8,256]{2,1,0:T(8,128)}, f32[32,8,256]{2,1,0:T(8,128)}, f32[27,8,256]{2,1,0:T(8,128)}, f32[27,8,256]{2,1,0:T(8,128)}) custom-call(f32[16,32,256]{2,1,0:T(8,128)} %all_to_all.10.in_ref), custom_call_target="tpu_custom_call" | custom-call | tf_op jit(solution)/shard_map/gather/pallas_call | solution.py:389
  19.8 5.2 %collective-permute-start = (f32[27,8,256]{2,1,0:T(8,128)}, f32[27,8,256]{2,1,0:T(8,128)S(1)}, u32[]{:S(2)}, u32[]{:S(2)}) collective-permute-start(f32[27,8,256]{2,1,0:T(8,128)} %get-tuple-element.20), channel_id=1, source_target_pairs={{0,2},{1,3},{2,4},{3,5},{4,6},{5,7},{6,8},{7,9},{8,10},{9,11},{10,... | collective-permute-start | bytes 663560 | tf_op jit(solution)/shard_map/ppermute | solution.py:406
  25.0 0.0 copy-start.8
  25.0 7.9 %collective-permute-start.1 = (f32[27,8,256]{2,1,0:T(8,128)}, f32[27,8,256]{2,1,0:T(8,128)S(1)}, u32[]{:S(2)}, u32[]{:S(2)}) collective-permute-start(f32[27,8,256]{2,1,0:T(8,128)} %get-tuple-element.22), channel_id=1, source_target_pairs={{2,0},{3,1},{4,2},{5,3},{6,4},{7,5},{8,6},{9,7},{10,8},{11,9},{12,... | collective-permute-start | bytes 663560 | tf_op jit(solution)/shard_map/ppermute | solution.py:407
  32.9 0.0 copy-done.8
  32.9 0.1 copy.4
  33.0 0.6 pad.4.tab_ref
  33.7 0.6 pad_add_fusion.scalars_ref
  34.2 2.8 %collective-permute-done.above_ref.cls_above_ref = f32[27,8,256]{2,1,0:T(8,128)S(1)} collective-permute-done((f32[27,8,256]{2,1,0:T(8,128)}, f32[27,8,256]{2,1,0:T(8,128)S(1)}, u32[]{:S(2)}, u32[]{:S(2)}) %collective-permute-start) | collective-permute-done | bytes 221216 | tf_op jit(solution)/shard_map/ppermute | solution.py:406
  37.1 0.0 copy-start
  37.1 4.9 %collective-permute-done.1.below_ref.cls_below_ref = f32[27,8,256]{2,1,0:T(8,128)S(1)} collective-permute-done((f32[27,8,256]{2,1,0:T(8,128)}, f32[27,8,256]{2,1,0:T(8,128)S(1)}, u32[]{:S(2)}, u32[]{:S(2)}) %collective-permute-start.1) | collective-permute-done | bytes 221216 | tf_op jit(solution)/shard_map/ppermute | solution.py:407
  41.9 0.0 copy-start.1
  41.9 0.0 copy-done
  41.9 0.7 copy-done.1
  42.6 17.4 %phase0.1 = (f32[2,32,128]{2,1,0:T(8,128)}, f32[32,8,256]{2,1,0:T(8,128)}, f32[27,8,256]{2,1,0:T(8,128)}, f32[27,8,256]{2,1,0:T(8,128)}) custom-call(s32[3]{0:T(128)} %pad_add_fusion.scalars_ref, f32[27,8,256]{2,1,0:T(8,128)} %copy-done, f32[32,8,256]{2,1,0:T(8,128)} %get-tuple-element.21.tile_ref, f32[27,8,256]{2,1,0:T(8,128)} %copy-done.1, ...), custom_call_target="tpu_custom_call" | custom-call | tf_op jit(solution)/shard_map/phase0/pallas_call | solution.py:427
  60.0 5.6 %collective-permute-start.2 = (f32[27,8,256]{2,1,0:T(8,128)}, f32[27,8,256]{2,1,0:T(8,128)S(1)}, u32[]{:S(2)}, u32[]{:S(2)}) collective-permute-start(f32[27,8,256]{2,1,0:T(8,128)} %get-tuple-element.25), channel_id=1, source_target_pairs={{0,2},{1,3},{2,4},{3,5},{4,6},{5,7},{6,8},{7,9},{8,10},{9,11},{10,... | collective-permute-start | bytes 663560 | tf_op jit(solution)/shard_map/ppermute | solution.py:406
  65.6 3.2 %collective-permute-start.3 = (f32[27,8,256]{2,1,0:T(8,128)}, f32[27,8,256]{2,1,0:T(8,128)S(1)}, u32[]{:S(2)}, u32[]{:S(2)}) collective-permute-start(f32[27,8,256]{2,1,0:T(8,128)} %get-tuple-element.27), channel_id=1, source_target_pairs={{2,0},{3,1},{4,2},{5,3},{6,4},{7,5},{8,6},{9,7},{10,8},{11,9},{12,... | collective-permute-start | bytes 663560 | tf_op jit(solution)/shard_map/ppermute | solution.py:407
  68.9 2.9 %collective-permute-done.2.above_ref = f32[27,8,256]{2,1,0:T(8,128)S(1)} collective-permute-done((f32[27,8,256]{2,1,0:T(8,128)}, f32[27,8,256]{2,1,0:T(8,128)S(1)}, u32[]{:S(2)}, u32[]{:S(2)}) %collective-permute-start.2) | collective-permute-done | bytes 221216 | tf_op jit(solution)/shard_map/ppermute | solution.py:406
  71.8 0.0 copy-start.2
  71.8 7.6 %collective-permute-done.3.below_ref = f32[27,8,256]{2,1,0:T(8,128)S(1)} collective-permute-done((f32[27,8,256]{2,1,0:T(8,128)}, f32[27,8,256]{2,1,0:T(8,128)S(1)}, u32[]{:S(2)}, u32[]{:S(2)}) %collective-permute-start.3) | collective-permute-done | bytes 221216 | tf_op jit(solution)/shard_map/ppermute | solution.py:407
  79.4 0.0 copy-start.3
  79.4 0.0 copy-done.2
  79.4 0.7 copy-done.3
  80.0 29.1 %phase1.1 = (f32[3,32,128]{2,1,0:T(8,128)}, f32[32,8,128]{2,1,0:T(8,128)}, f32[27,8,128]{2,1,0:T(8,128)}, f32[27,8,128]{2,1,0:T(8,128)}) custom-call(s32[3]{0:T(128)} %pad_add_fusion.scalars_ref, f32[27,8,256]{2,1,0:T(8,128)} %copy-done.2, f32[32,8,256]{2,1,0:T(8,128)} %get-tuple-element.26.tile_ref, f32[27,8,256]{2,1,0:T(8,128)} %copy-done.3, ...), custom_call_target="tpu_custom_call" | custom-call | tf_op jit(solution)/shard_map/phase1/pallas_call | solution.py:427
  109.2 5.5 %collective-permute-start.4 = (f32[27,8,128]{2,1,0:T(8,128)}, f32[27,8,128]{2,1,0:T(8,128)S(1)}, u32[]{:S(2)}, u32[]{:S(2)}) collective-permute-start(f32[27,8,128]{2,1,0:T(8,128)} %get-tuple-element.29), channel_id=1, source_target_pairs={{0,2},{1,3},{2,4},{3,5},{4,6},{5,7},{6,8},{7,9},{8,10},{9,11},{10,... | collective-permute-start | bytes 331784 | tf_op jit(solution)/shard_map/ppermute | solution.py:406
  114.7 3.3 %collective-permute-start.5 = (f32[27,8,128]{2,1,0:T(8,128)}, f32[27,8,128]{2,1,0:T(8,128)S(1)}, u32[]{:S(2)}, u32[]{:S(2)}) collective-permute-start(f32[27,8,128]{2,1,0:T(8,128)} %get-tuple-element.31), channel_id=1, source_target_pairs={{2,0},{3,1},{4,2},{5,3},{6,4},{7,5},{8,6},{9,7},{10,8},{11,9},{12,... | collective-permute-start | bytes 331784 | tf_op jit(solution)/shard_map/ppermute | solution.py:407
  118.0 1.9 %narrow.1 = (f32[9,8,128]{2,1,0:T(8,128)}, f32[32,8,128]{2,1,0:T(8,128)}, f32[9,8,128]{2,1,0:T(8,128)}) custom-call(f32[27,8,256]{2,1,0:T(8,128)} %copy-done, f32[32,8,256]{2,1,0:T(8,128)} %get-tuple-element.23.cls_ref.own_ref, f32[27,8,256]{2,1,0:T(8,128)} %copy-done.1), custom_call_target="tpu_custom_call" | custom-call | tf_op jit(solution)/shard_map/narrow/pallas_call | solution.py:411
  120.0 0.0 collective-permute-done.4.above_ref
  120.0 0.0 copy-start.4
  120.0 2.6 %collective-permute-done.5.below_ref = f32[27,8,128]{2,1,0:T(8,128)S(1)} collective-permute-done((f32[27,8,128]{2,1,0:T(8,128)}, f32[27,8,128]{2,1,0:T(8,128)S(1)}, u32[]{:S(2)}, u32[]{:S(2)}) %collective-permute-start.5) | collective-permute-done | bytes 110624 | tf_op jit(solution)/shard_map/ppermute | solution.py:407
  122.6 0.0 copy-start.5
  122.6 0.0 copy-done.4
  122.6 0.6 copy-done.5
  123.2 0.0 copy-start.6
  123.2 0.0 copy-start.7
  123.2 19.6 %phase2.1 = f32[3,32,128]{2,1,0:T(8,128)} custom-call(s32[3]{0:T(128)} %pad_add_fusion.scalars_ref, f32[27,8,128]{2,1,0:T(8,128)} %copy-done.4, f32[32,8,128]{2,1,0:T(8,128)} %get-tuple-element.30.tile_ref, f32[27,8,128]{2,1,0:T(8,128)} %copy-done.5, f32[9,8,128]{2,1,0:T(8,128)} %get-tuple-element.32.cls_above_ref, f32[32,8,128]{2,1,0:T(8,128)} %get-tuple-element.33.cls_ref, ...), custom_call_target="tpu_custom_call" | custom-call | tf_op jit(solution)/shard_map/phase2/pallas_call | solution.py:427
  142.8 0.0 copy-done.6
  142.8 0.0 copy-done.7
  142.8 0.8 pad_maximum_fusion
  143.7 9.8 %all_to_all.11.in_ref = f32[16,16,128]{2,1,0:T(8,128)} all-to-all(f32[16,16,128]{2,1,0:T(8,128)S(1)} %bitcast.9), channel_id=1, replica_groups={{0,1,64,65,128,129,192,193,256,257,320,321,384,385,448,449},{2,3,66,67,..., dimensions={0} | all-to-all | bytes 262144 | tf_op jit(solution)/shard_map/all_to_all | solution.py:439
  153.5 1.6 %collect.1 = f32[1,16,1024]{2,1,0:T(8,128)} custom-call(f32[16,16,128]{2,1,0:T(8,128)} %all_to_all.11.in_ref), custom_call_target="tpu_custom_call" | custom-call | tf_op jit(solution)/shard_map/collect/pallas_call | solution.py:440
Async XLA Ops:
  19.8 17.2 %collective-permute-start = (f32[27,8,256]{2,1,0:T(8,128)}, f32[27,8,256]{2,1,0:T(8,128)S(1)}, u32[]{:S(2)}, u32[]{:S(2)}) collective-permute-start(f32[27,8,256]{2,1,0:T(8,128)} %get-tuple-element.20), channel_id=1, source_target_pairs={{0,2},{1,3},{2,4},{3,5},{4,6},{5,7},{6,8},{7,9},{8,10},{9,11},{10,... | collective-permute-start | bytes 663560 | tf_op jit(solution)/shard_map/ppermute | solution.py:406
  25.0 7.9 %copy-start.8 = (f32[2,8,2,10]{3,2,1,0:T(2,128)S(1)}, f32[2,8,2,10]{3,2,1,0:T(2,128)}, u32[]{:S(2)}) copy-start(f32[2,8,2,10]{3,2,1,0:T(2,128)} %param.5) | copy-start | bytes 3844
  25.0 16.9 %collective-permute-start.1 = (f32[27,8,256]{2,1,0:T(8,128)}, f32[27,8,256]{2,1,0:T(8,128)S(1)}, u32[]{:S(2)}, u32[]{:S(2)}) collective-permute-start(f32[27,8,256]{2,1,0:T(8,128)} %get-tuple-element.22), channel_id=1, source_target_pairs={{2,0},{3,1},{4,2},{5,3},{6,4},{7,5},{8,6},{9,7},{10,8},{11,9},{12,... | collective-permute-start | bytes 663560 | tf_op jit(solution)/shard_map/ppermute | solution.py:407
  37.1 4.9 %copy-start = (f32[27,8,256]{2,1,0:T(8,128)}, f32[27,8,256]{2,1,0:T(8,128)S(1)}, u32[]{:S(2)}) copy-start(f32[27,8,256]{2,1,0:T(8,128)S(1)} %collective-permute-done.above_ref.cls_above_ref) | copy-start | bytes 663556
  41.9 0.7 copy-start.1
  60.0 11.8 %collective-permute-start.2 = (f32[27,8,256]{2,1,0:T(8,128)}, f32[27,8,256]{2,1,0:T(8,128)S(1)}, u32[]{:S(2)}, u32[]{:S(2)}) collective-permute-start(f32[27,8,256]{2,1,0:T(8,128)} %get-tuple-element.25), channel_id=1, source_target_pairs={{0,2},{1,3},{2,4},{3,5},{4,6},{5,7},{6,8},{7,9},{8,10},{9,11},{10,... | collective-permute-start | bytes 663560 | tf_op jit(solution)/shard_map/ppermute | solution.py:406
  65.6 13.7 %collective-permute-start.3 = (f32[27,8,256]{2,1,0:T(8,128)}, f32[27,8,256]{2,1,0:T(8,128)S(1)}, u32[]{:S(2)}, u32[]{:S(2)}) collective-permute-start(f32[27,8,256]{2,1,0:T(8,128)} %get-tuple-element.27), channel_id=1, source_target_pairs={{2,0},{3,1},{4,2},{5,3},{6,4},{7,5},{8,6},{9,7},{10,8},{11,9},{12,... | collective-permute-start | bytes 663560 | tf_op jit(solution)/shard_map/ppermute | solution.py:407
  71.8 7.6 %copy-start.2 = (f32[27,8,256]{2,1,0:T(8,128)}, f32[27,8,256]{2,1,0:T(8,128)S(1)}, u32[]{:S(2)}) copy-start(f32[27,8,256]{2,1,0:T(8,128)S(1)} %collective-permute-done.2.above_ref) | copy-start | bytes 663556
  79.4 0.7 copy-start.3
  109.2 10.8 %collective-permute-start.4 = (f32[27,8,128]{2,1,0:T(8,128)}, f32[27,8,128]{2,1,0:T(8,128)S(1)}, u32[]{:S(2)}, u32[]{:S(2)}) collective-permute-start(f32[27,8,128]{2,1,0:T(8,128)} %get-tuple-element.29), channel_id=1, source_target_pairs={{0,2},{1,3},{2,4},{3,5},{4,6},{5,7},{6,8},{7,9},{8,10},{9,11},{10,... | collective-permute-start | bytes 331784 | tf_op jit(solution)/shard_map/ppermute | solution.py:406
  114.7 7.9 %collective-permute-start.5 = (f32[27,8,128]{2,1,0:T(8,128)}, f32[27,8,128]{2,1,0:T(8,128)S(1)}, u32[]{:S(2)}, u32[]{:S(2)}) collective-permute-start(f32[27,8,128]{2,1,0:T(8,128)} %get-tuple-element.31), channel_id=1, source_target_pairs={{2,0},{3,1},{4,2},{5,3},{6,4},{7,5},{8,6},{9,7},{10,8},{11,9},{12,... | collective-permute-start | bytes 331784 | tf_op jit(solution)/shard_map/ppermute | solution.py:407
  120.0 2.6 %copy-start.4 = (f32[27,8,128]{2,1,0:T(8,128)}, f32[27,8,128]{2,1,0:T(8,128)S(1)}, u32[]{:S(2)}) copy-start(f32[27,8,128]{2,1,0:T(8,128)S(1)} %collective-permute-done.4.above_ref) | copy-start | bytes 331780
  122.6 0.6 copy-start.5
  123.2 19.6 %copy-start.6 = (f32[3,32,128]{2,1,0:T(8,128)S(1)}, f32[3,32,128]{2,1,0:T(8,128)}, u32[]{:S(2)}) copy-start(f32[3,32,128]{2,1,0:T(8,128)} %get-tuple-element.28) | copy-start | bytes 147460
  123.2 19.6 %copy-start.7 = (f32[2,32,128]{2,1,0:T(8,128)S(1)}, f32[2,32,128]{2,1,0:T(8,128)}, u32[]{:S(2)}) copy-start(f32[2,32,128]{2,1,0:T(8,128)} %get-tuple-element.24) | copy-start | bytes 98308
